TPU v7x, 128 devices: a whole 4x4x4 slice. The times are simulated.
128 devices in a mesh: blk: 64 (over z, y_lo, x, core), span: 2 (over y_hi).
Axes of the slice: x: 4, y: 4 (y_hi: 2, y_lo: 2; y = y_hi * 2 + y_lo), z: 4, core: 2. Of those that a mesh axis runs over, the one named last changes fastest.
Arguments:
- state_now: float32 [5, 9, 16, 1024, 128], P(None, None, 'span', 'blk'), may hold values from -6 to 6
- base_state: float32 [5, 9, 16, 1024, 128], P(None, None, 'span', 'blk'), may hold values from -6 to 6
- time_step: float32 [16, 1024, 128], P('span', 'blk'), may hold values from 0.05 to 0.3
- row_map: int32 [64], replicated, may hold values from 0 to 2, as said below
- lag_shift: int32 [3], replicated, may hold values from 1 to 8
- mode_count: int32 [2], replicated, may hold values from 8 to 16, as said below
- jacobian: float32 [3, 3, 5, 5], replicated, may hold values from -2.5 to 2.5
- dissipation: float32 [3, 3], replicated, may hold values from 0.2 to 1
- frequency: float32 [3], replicated, may hold values from 0.5 to 2
Outputs:
- state_next: float32 [5, 9, 16, 1024, 128], P(None, None, 'span', 'blk')
Inputs may be any that keep to these rules, and one draw needn't show every extreme that they name: `row_map`: never falling; the 3 rows hold 2, 33 and the remaining blocks, in an order that varies. `mode_count`: one interface keeps exactly 16 modes.
All inputs are finite; a program needn't handle non-finite values.
Results may differ from a plain program's by a relative error of at most 0.00005.
Values sent between devices are 32-bit elements; how exact they have to be, the bound alone decides.
No kernel may reach another device: no remote copies, remote signals or barrier semaphores. Data moves between devices by JAX's collectives and lax.ppermute only.
A program may use at most 192 MiB of HBM per device.

v0:
```python
import functools
import math

import jax
import jax.numpy as jnp
from jax import lax
from jax.experimental import pallas as pl
from jax.experimental.pallas import tpu as pltpu
from jax.sharding import Mesh
from jax.sharding import PartitionSpec as P

BLK = ("blk_0", "blk_1", "blk_2", "blk_3")
ORDERS = ((2, 33, 29), (2, 29, 33), (33, 2, 29), (33, 29, 2), (29, 2, 33), (29, 33, 2))
EXACT = lax.Precision.HIGHEST
VMEM = pltpu.VMEM
F32 = jnp.float32
QUAD = (0, 1, 8, 9)
HOPS = (2, 6, 16, 48)
DN = tuple(0.5 * math.cos(math.pi * n) / math.sin(math.pi * n / 9) for n in range(5) if n)


ALONG = ((0, 5), (5, 8))
ACROSS = ((0, 2), (2, 8))
CENTRE, WAVE, SPAN, COEFS = 90, 91, 95, 97


def vspec():
    return pl.BlockSpec(memory_space=VMEM)


def sspec():
    return pl.BlockSpec(memory_space=pltpu.SMEM)


def hspec():
    return pl.BlockSpec(memory_space=pltpu.HBM)


def own_block():
    return (
        (lax.axis_index("blk_0") * 2 + lax.axis_index("blk_1")) * 4 + lax.axis_index("blk_2")
    ) * 2 + lax.axis_index("blk_3")


def own_quarter():
    return lax.axis_index("blk_1") * 2 + lax.axis_index("blk_3")


def lengths_of(order):
    n0 = jnp.where(order < 2, 2, jnp.where(order < 4, 33, 29))
    n1 = jnp.where(
        (order == 2) | (order == 4), 2, jnp.where((order == 0) | (order == 5), 33, 29)
    )
    return n0, n1


def place_in_row(order, block):
    n0, n1 = lengths_of(order)
    row = (block >= n0).astype(jnp.int32) + (block >= n0 + n1).astype(jnp.int32)
    begin = jnp.where(row == 0, 0, jnp.where(row == 1, n0, n0 + n1))
    total = jnp.where(row == 0, n0, jnp.where(row == 1, n1, 64 - n0 - n1))
    return row, block - begin, total


def sine_and_cosine(count, period):
    inverse = 1.0 / period
    rest = count - jnp.floor(count * inverse + 0.5) * period
    quarters = rest * (4.0 * inverse)
    turn = jnp.floor(quarters + 0.5)
    z = (quarters - turn) * (0.5 * math.pi)
    y = z * z
    sin = z * (1.0 + y * (-1 / 6 + y * (1 / 120 + y * (-1 / 5040 + y * (1 / 362880)))))
    cos = 1.0 + y * (
        -1 / 2 + y * (1 / 24 + y * (-1 / 720 + y * (1 / 40320 + y * (-1 / 3628800))))
    )
    turn = turn.astype(jnp.int32) & 3
    odd = (turn & 1) == 1
    sin, cos = jnp.where(odd, cos, sin), jnp.where(odd, sin, cos)
    return jnp.where(turn >= 2, -sin, sin), jnp.where((turn == 1) | (turn == 2), -cos, cos)


def order_of(rows):
    late = rows[31] == 2
    first = jnp.where(rows[2] == 1, 0, jnp.where(rows[29] == 0, 2, 4))
    second = jnp.where(
        first == 0,
        late.astype(jnp.int32),
        jnp.where(first == 2, (rows[35] != 2).astype(jnp.int32), 1 - late.astype(jnp.int32)),
    )
    return first + second


def waves(members):
    shape = (16, 128)
    lane = lax.broadcasted_iota(jnp.int32, shape, 1)
    mode = lax.broadcasted_iota(jnp.int32, shape, 0)
    member = (lane // 16) & 3

    def pick(n):
        values = [jnp.full(shape, m[n], jnp.int32) for m in members]
        return jnp.where(
            member < 2,
            jnp.where(member == 0, values[0], values[1]),
            jnp.where(member == 2, values[2], values[3]),
        )

    its_row = pick(0)
    period = (pick(2) * 32).astype(F32)
    odd = ((pick(1) * 16 + (lane & 15)) * 2 + 1).astype(F32)
    sin, cos = sine_and_cosine(mode.astype(F32) * odd, period)
    return its_row, lane, mode, period, cos, sin


def members_of(order):
    block = own_block()
    return [place_in_row(order, lax.bitwise_xor(block, m)) for m in QUAD]


def write_forward(members, forward):
    its_row, _, mode, period, cos, sin = waves(members)
    weight = jnp.where(mode == 0, 2.0, 4.0) / period
    for r in range(3):
        here = its_row == r
        forward[pl.ds(32 * r, 16), :] = jnp.where(here, cos * weight, 0.0)[:, :64]
        forward[pl.ds(32 * r + 16, 16), :] = jnp.where(here, sin * weight, 0.0)[:, :64]


def write_rest(members, count, dis, freq, jac, backward, mixing, coef):
    row = members[0][0]
    its_row, lane, mode, _, cos, sin = waves(members)
    seen = its_row - jnp.where(lane < 64, 1, 0)
    back = []
    for gap in range(2):
        kept = (seen == gap) & (mode < count[gap])
        back += [jnp.where(kept, cos, 0.0), jnp.where(kept, sin, 0.0)]
    backward[...] = jnp.concatenate(back, axis=0).T

    shape = (128, 128)
    source = lax.broadcasted_iota(jnp.int32, shape, 0)
    target = lax.broadcasted_iota(jnp.int32, shape, 1)

    def variable(ids):
        return sum((ids >= 18 * n).astype(jnp.int32) for n in range(1, 5))

    line = lax.broadcasted_iota(jnp.int32, (8, 128), 1)
    u_of = variable(line)
    v_of = variable(lax.broadcasted_iota(jnp.int32, (128, 1), 0))
    crossed = lax.bitwise_xor(target, 1)
    same = (crossed - 18 * u_of[:1]) == (source - 18 * v_of)
    terms = jnp.zeros(shape, F32)
    for v in range(5):
        entries = jnp.zeros((8, 128), F32)
        for u in range(5):
            entries = jnp.where(u_of == u, jac[row, u, 1, v], entries)
        terms = jnp.where(v_of == v, entries[:1], terms)
    terms = terms * jnp.where((source & 1) == 0, -0.5, 0.5)
    terms = terms - jnp.where(crossed == source, dis[row, 1], 0.0)
    mixing[...] = jnp.where(same & (source < 90), terms, 0.0)

    def put(at, value):
        coef[at] = jnp.full((8, 128), value, F32)

    for d in range(3):
        for u in range(5):
            for v in range(5):
                half = 0.5 * jac[row, u, d, v]
                if u == v:
                    put(75 + d * 5 + u, half - dis[row, d])
                    put(d * 25 + u * 5 + v, half + dis[row, d])
                else:
                    put(d * 25 + u * 5 + v, half)
    put(CENTRE, 2.0 * (dis[row, 0] + dis[row, 1] + dis[row, 2]))
    for n in range(4):
        put(WAVE + n, freq[row] * DN[n])
    upper = lax.axis_index("span")
    put(SPAN, upper.astype(F32))
    put(SPAN + 1, (1 - upper).astype(F32))


def faces_kernel(x_hbm, f0, f1, f2, f3, faces, x, sem):
    copies = [
        pltpu.make_async_copy(
            x_hbm.at[:, pl.ds(16 * s, 16), :], x.at[:, pl.ds(24 * s + 32, 16), :], sem.at[s]
        )
        for s in range(8)
    ]
    for copy in copies:
        copy.start()
    lane = lax.broadcasted_iota(jnp.int32, (8, 128), 1) // 2
    for s in range(8):
        copies[s].wait()
        acc = [jnp.zeros((8, 128), F32) for _ in range(2)]
        for j in range(45):
            for h in range(2):
                turned = pltpu.roll(x[j, pl.ds(24 * s + 32 + 8 * h, 8), :], 2 * j + 1, 1)
                acc[h] = jnp.where(lane == j, turned, acc[h])
        for h in range(2):
            faces[s, pl.ds(8 * h, 8), :] = acc[h]
    q = own_quarter()
    for d, ref in enumerate((f0, f1, f2, f3)):
        ref[...] = faces[pl.ds(2 * lax.bitwise_xor(q, d), 2)]


def leave_kernel(
    rows_hbm, lag_hbm, x, order_ref, rim_l, rim_r, edge, forward, rows, lag, sem
):
    small = [
        pltpu.make_async_copy(a, b, sem.at[n])
        for n, (a, b) in enumerate(((rows_hbm, rows), (lag_hbm, lag)))
    ]
    for copy in small:
        copy.start()
    outer = pl.multiple_of(jnp.where(lax.axis_index("span") == 0, 200, 32), 8)

    @pl.loop(0, 9)
    def _(k):
        for v in range(5):
            edge[v * 9 + k] = x[v * 9 + k, pl.ds(outer, 16), :]

    for copy in small:
        copy.wait()
    order = order_of(rows)
    order_ref[0] = order
    members = members_of(order)
    write_forward(members, forward)
    row, position, total = members[0]
    turn_left = jnp.where(position == 0, 9 - lag[row], 0)
    turn_right = jnp.where(position == total - 1, lag[row], 0)

    @pl.loop(0, 9)
    def _(k):
        for v in range(5):
            j = v * 9 + k
            rim_l[j] = x[v * 9 + lax.rem(k + turn_left, 9), pl.ds(32, 8, stride=24), :]
            rim_r[j] = x[v * 9 + lax.rem(k + turn_right, 9), pl.ds(47, 8, stride=24), :]


def tables_kernel(
    rows_hbm, count_hbm, dis_hbm, freq_hbm, jac_hbm, x_hbm,
    x, backward, mixing, coef, rows, count, dis, freq, jac, sem, sem_x,
):
    small = [
        pltpu.make_async_copy(a, b, sem.at[n])
        for n, (a, b) in enumerate(
            (
                (rows_hbm, rows), (count_hbm, count),
                (dis_hbm, dis), (freq_hbm, freq), (jac_hbm, jac),
            )
        )
    ]
    copies = [
        pltpu.make_async_copy(
            x_hbm.at[:, pl.ds(16 * s, 16), :], x.at[:, pl.ds(24 * s + 32, 16), :], sem_x.at[s]
        )
        for s in range(8)
    ]
    for copy in small + copies:
        copy.start()
    for copy in small:
        copy.wait()
    write_rest(members_of(order_of(rows)), count, dis, freq, jac, backward, mixing, coef)
    for copy in copies:
        copy.wait()


def project_kernel(f0, f1, f2, f3, forward, out):
    even = lax.broadcasted_iota(jnp.int32, (32, 128), 1) % 2 == 0
    for i in range(2):
        columns = jnp.concatenate([f0[i], f1[i], f2[i], f3[i]], axis=0)
        parts = jnp.dot(forward[...], columns, precision=EXACT, preferred_element_type=F32)
        low, mid, high = parts[:32], parts[32:64], parts[64:]
        out[i, pl.ds(0, 32), :] = jnp.where(even, low, mid)
        out[i, pl.ds(32, 32), :] = jnp.where(even, mid, high)


def evaluate_kernel(m0, m1, backward, g0, g1, g2, g3):
    even = lax.broadcasted_iota(jnp.int32, (64, 128), 1) % 2 == 0
    for i in range(2):
        modes = m0[i] + m1[i]
        both = jnp.dot(backward[...], modes, precision=EXACT, preferred_element_type=F32)
        ghost = jnp.where(even, both[:64], both[64:])
        for d, ref in enumerate((g0, g1, g2, g3)):
            ref[i] = ghost[16 * d : 16 * d + 16]


def ghosts_kernel(coef, ghost_l, ghost_r, edge, x_in, x):
    keep_low = jnp.concatenate([coef[SPAN]] * 2, axis=0)
    keep_high = jnp.concatenate([coef[SPAN + 1]] * 2, axis=0)

    @pl.loop(0, 9)
    def _(k):
        for v in range(5):
            j = v * 9 + k
            x[j, pl.ds(31, 8, stride=24), :] = ghost_l[j]
            x[j, pl.ds(48, 8, stride=24), :] = ghost_r[j]
            x[j, pl.ds(8, 16), :] = edge[j] * keep_low
            x[j, pl.ds(224, 16), :] = edge[j] * keep_high


def across_kernel(first, last, coef, x, dt, base, out_in, out):
    @pl.loop(first, last)
    def _(s):
        at = pl.multiple_of(24 * s + 32, 8)
        to = pl.multiple_of(16 * s, 16)
        for h in range(2):
            there = pl.ds(to + 8 * h, 8)
            step = dt[there, :]
            for k in range(9):
                acc, diffs = [], []
                for v in range(5):
                    j = v * 9 + k
                    pairs = [
                        (d, x[j, pl.ds(at + 8 * h + r, 8), :], x[j, pl.ds(at + 8 * h - r, 8), :])
                        for d, r in ((0, 1), (2, 24))
                    ]
                    diffs.append({d: plus - minus for d, plus, minus in pairs})
                    terms = [
                        plus * coef[75 + d * 5 + v] - minus * coef[d * 25 + v * 6]
                        for d, plus, minus in pairs
                    ]
                    acc.append(terms[0] + terms[1])
                for u in range(5):
                    j = u * 9 + k
                    total_u = out[j, there, :] + acc[u]
                    for d in (0, 2):
                        part = None
                        for v in range(5):
                            if v != u:
                                product = diffs[v][d] * coef[d * 25 + u * 5 + v]
                                part = product if part is None else part + product
                        total_u = total_u + part
                    out[j, there, :] = base[j, there, :] - step * total_u


def along_first_kernel(first, last, coef, x, base_hbm, out, base, sem):
    fetch = pltpu.make_async_copy(base_hbm, base, sem)
    fetch.start()
    along_kernel(first, last, coef, x, out)
    fetch.wait()


def along_kernel(first, last, coef, x, *refs):
    out = refs[-1]

    @pl.loop(first, last)
    def _(s):
        at = pl.multiple_of(24 * s + 32, 8)
        to = pl.multiple_of(16 * s, 16)
        for h in range(2):
            here, there = pl.ds(at + 8 * h, 8), pl.ds(to + 8 * h, 8)
            for u in range(5):
                line = [x[u * 9 + k, here, :] for k in range(9)]
                for k in range(9):
                    turn = [
                        (line[(k - n) % 9] - line[(k + n) % 9]) * coef[WAVE + n - 1]
                        for n in range(1, 5)
                    ]
                    turn.append(line[k] * coef[CENTRE])
                    out[u * 9 + k, there, :] = (turn[0] + turn[1]) + (turn[2] + turn[3]) + turn[4]
            for k in range(9):
                acc, diffs = [], []
                for v in range(5):
                    j = v * 9 + k
                    own = x[j, here, :]
                    plus, minus = pltpu.roll(own, 127, 1), pltpu.roll(own, 1, 1)
                    diffs.append(plus - minus)
                    acc.append(
                        out[j, there, :]
                        + (plus * coef[80 + v] - minus * coef[25 + v * 6])
                    )
                for u in range(5):
                    part = None
                    for v in range(5):
                        if v != u:
                            product = diffs[v] * coef[25 + u * 5 + v]
                            part = product if part is None else part + product
                    out[u * 9 + k, there, :] = acc[u] + part


def finish_kernel(acc, g0, g1, g2, g3, faces, mixing, dt, out_hbm, out, ghost, sem):
    q = own_quarter()
    for d, ref in enumerate((g0, g1, g2, g3)):
        for i in range(2):
            s = 2 * lax.bitwise_xor(q, d) + i
            ghost[pl.ds(pl.multiple_of(16 * s, 16), 16), :] = ref[i] - faces[s]
    terms = jnp.dot(ghost[...], mixing[...], precision=EXACT, preferred_element_type=F32)
    lane = lax.broadcasted_iota(jnp.int32, (128, 128), 1)
    step = jnp.where((lane == 0) | (lane == 127), dt[...], 0.0)
    for v in range(5):
        @pl.loop(9 * v, 9 * v + 9, step=3)
        def _(first):
            for j in (first, first + 1, first + 2):
                turned = pltpu.roll(terms, 127 - 2 * j, 1)
                out[j] = acc[j] - step * turned

        pltpu.make_async_copy(
            out.at[pl.ds(9 * v, 9)], out_hbm.at[pl.ds(9 * v, 9)], sem.at[v]
        ).start()
    for v in range(5):
        pltpu.make_async_copy(
            out.at[pl.ds(9 * v, 9)], out_hbm.at[pl.ds(9 * v, 9)], sem.at[v]
        ).wait()


def swap(x, mask):
    return lax.ppermute(x, BLK, [(i, i ^ mask) for i in range(64)])


def ring(order):
    pairs, begin = [], 0
    for length in order:
        pairs += [(begin + i, begin + (i + 1) % length) for i in range(length)]
        begin += length
    return pairs


def ring_swaps(order):
    right = ring(order)
    left = [(t, s) for s, t in right]

    def run(rim_l, rim_r):
        return lax.ppermute(rim_r, BLK, right), lax.ppermute(rim_l, BLK, left)

    return run


def sds(*shape, dtype=F32):
    return jax.ShapeDtypeStruct(shape, dtype)


def call(kernel, outs, in_specs, out_specs, scratch=(), limit=8, flops=0, aliases={}):
    return pl.pallas_call(
        kernel,
        out_shape=outs,
        in_specs=in_specs,
        out_specs=out_specs,
        scratch_shapes=list(scratch),
        input_output_aliases=aliases,
        cost_estimate=pl.CostEstimate(flops=flops, bytes_accessed=flops // 8, transcendentals=0),
        compiler_params=pltpu.CompilerParams(vmem_limit_bytes=limit << 20),
    )


def per_device(state, base, dt, row_map, lag, count, jac, dis, freq):
    shape = state.shape
    x = state.reshape(45, 128, 128)
    b = base.reshape(45, 128, 128)
    dt = dt.reshape(128, 128)
    jac = jac.transpose(0, 2, 1, 3)
    x, b, row_map, lag, count, dis, freq, jac = [
        pltpu.with_memory_space_constraint(a, pltpu.HBM)
        for a in (x, b, row_map, lag, count, dis, freq, jac)
    ]
    quarter, rim = sds(2, 16, 128), sds(45, 8, 128)
    padded, whole = VMEM((45, 240, 128), F32), VMEM((45, 128, 128), F32)
    dma = pltpu.SemaphoreType.DMA
    x_hbm = x
    f0, f1, f2, f3, faces, x = call(
        faces_kernel,
        [quarter] * 4 + [sds(8, 16, 128), padded],
        [hspec()],
        [vspec()] * 6,
        [dma((8,))],
    )(x)
    r = []
    for d, f in ((1, f1), (2, f2), (3, f3)):
        r.append(swap(f, QUAD[d]))
    order, rim_l, rim_r, edge, forward = call(
        leave_kernel,
        [sds(1, dtype=jnp.int32), rim, rim, sds(45, 16, 128), sds(96, 64)],
        [hspec()] * 2 + [vspec()],
        [sspec()] + [vspec()] * 4,
        [pltpu.SMEM((64,), jnp.int32), pltpu.SMEM((3,), jnp.int32), dma((2,))],
        flops=2000000,
    )(row_map, lag, x)
    from_span = lax.ppermute(edge, "span", [(0, 1), (1, 0)])
    modes = call(
        project_kernel, sds(2, 64, 128), [vspec()] * 5, vspec(), flops=1000000
    )(f0, *r, forward)
    from_left, from_right = lax.switch(
        order[0], [ring_swaps(lengths) for lengths in ORDERS], rim_l, rim_r
    )
    for n, mask in enumerate(HOPS):
        other = swap(modes, mask)
        if n < 3:
            modes = modes + other
    x, backward, mixing, coef = call(
        tables_kernel,
        [padded, sds(128, 64), sds(128, 128), sds(COEFS, 8, 128)],
        [hspec()] * 6,
        [vspec()] * 4,
        [
            pltpu.SMEM((64,), jnp.int32),
            pltpu.SMEM((2,), jnp.int32),
            pltpu.SMEM((3, 3), F32),
            pltpu.SMEM((3,), F32),
            pltpu.SMEM((3, 5, 3, 5), F32),
            dma((5,)),
            dma((8,)),
        ],
        flops=3000000,
    )(row_map, count, dis, freq, jac, x_hbm)
    acc, b = call(
        functools.partial(along_first_kernel, *ALONG[0]),
        [whole, whole],
        [vspec()] * 2 + [hspec()],
        [vspec()] * 2,
        [dma],
        flops=10000000,
    )(coef, x, b)
    for first, last in ALONG[1:]:
        acc = call(
            functools.partial(along_kernel, first, last),
            whole,
            [vspec()] * 3,
            vspec(),
            flops=3000000 * (last - first),
            aliases={2: 0},
        )(coef, x, acc)
    x = call(
        ghosts_kernel, padded, [vspec()] * 5, vspec(), flops=1000000, aliases={4: 0}
    )(coef, from_left, from_right, from_span, x)
    for first, last in ACROSS:
        acc = call(
            functools.partial(across_kernel, first, last),
            whole,
            [vspec()] * 5,
            vspec(),
            flops=5000000 * (last - first),
            aliases={4: 0},
        )(coef, x, dt, b, acc)
    g = call(
        evaluate_kernel, [quarter] * 4, [vspec()] * 3, [vspec()] * 4, flops=1000000
    )(modes, other, backward)
    h = []
    for d in (1, 2, 3):
        h.append(swap(g[d], QUAD[d]))
    out = call(
        finish_kernel,
        sds(45, 128, 128),
        [vspec()] * 8,
        hspec(),
        [VMEM((45, 128, 128), F32), VMEM((128, 128), F32), dma((5,))],
        flops=10000000,
    )(acc, g[0], *h, faces, mixing, dt)
    return out.reshape(shape)


def solution(mesh):
    finer = Mesh(
        mesh.devices.reshape(4, 2, 4, 2, mesh.shape["span"]),
        ("blk_0", "blk_1", "blk_2", "blk_3", "span"),
    )
    return jax.shard_map(
        per_device,
        mesh=finer,
        in_specs=(
            P(None, None, "span", BLK, None),
            P(None, None, "span", BLK, None),
            P("span", BLK, None),
            P(),
            P(),
            P(),
            P(),
            P(),
            P(),
        ),
        out_specs=P(None, None, "span", BLK, None),
        check_vma=False,
    )
```

profile of v0, /device:TPU:1, one launch (start us, length us, event | category | flops | bytes accessed | tf_op | source)
XLA Modules:
  0.0 62.8 jit_solution(10236633523661413259)
XLA Ops:
  0.0 2.4 %shard_map.92 = (f32[2,16,128]{2,1,0:T(8,128)S(1)}, f32[2,16,128]{2,1,0:T(8,128)S(1)}, f32[2,16,128]{2,1,0:T(8,128)S(1)}, f32[2,16,128]{2,1,0:T(8,128)S(1)}, f32...) custom-call(f32[45,128,128]{2,1,0:T(8,128)} %bitcast.9), custom_call_target="tpu_custom_call" | custom-call | tf_op jit(solution)/shard_map/pallas_call | solution.py:458
  2.4 1.4 %shard_map.93 = (s32[1]{0:T(128)}, f32[45,8,128]{2,1,0:T(8,128)S(1)}, f32[45,8,128]{2,1,0:T(8,128)S(1)}, f32[45,16,128]{2,1,0:T(8,128)S(1)}, f32[96,64]{1,0:T(8,128)S(1)}) custom-call(s32[64]{0:T(128)} %rows_hbm.3, s32[3]{0:T(128)} %lag_hbm.1, f32[45,240,128]{2,1,0:T(8,128)S(1)} %get-tuple-element.65.x), custom_call_target="tpu_custom_call" | custom-call | flops 2000000 | bytes 250000 | tf_op jit(solution)/shard_map/pallas_call | solution.py:468
  3.8 3.8 %collective-permute-start.12 = (f32[45,16,128]{2,1,0:T(8,128)S(1)}, f32[45,16,128]{2,1,0:T(8,128)S(1)}, u32[]{:S(2)}, u32[]{:S(2)}) collective-permute-start(f32[45,16,128]{2,1,0:T(8,128)S(1)} %get-tuple-element.71), channel_id=1, source_target_pairs={{0,1},{1,0},{2,3},{3,2},{4,5},{5,4},{6,7},{7,6},{8,9},{9,8},{10,11... | collective-permute-start | bytes 1105928 | tf_op jit(solution)/shard_map/ppermute | solution.py:476
  7.6 1.0 %collective-permute-start.13 = (f32[2,16,128]{2,1,0:T(8,128)S(1)}, f32[2,16,128]{2,1,0:T(8,128)S(1)}, u32[]{:S(2)}, u32[]{:S(2)}) collective-permute-start(f32[2,16,128]{2,1,0:T(8,128)S(1)} %get-tuple-element.76), channel_id=1, source_target_pairs={{0,2},{2,0},{4,6},{6,4},{8,10},{10,8},{12,14},{14,12},{16,18},{18,... | collective-permute-start | bytes 49160 | tf_op jit(solution)/shard_map/ppermute | solution.py:406
  8.6 0.4 collective-permute-start.14
  9.0 1.2 %collective-permute-start.15 = (f32[2,16,128]{2,1,0:T(8,128)S(1)}, f32[2,16,128]{2,1,0:T(8,128)S(1)}, u32[]{:S(2)}, u32[]{:S(2)}) collective-permute-start(f32[2,16,128]{2,1,0:T(8,128)S(1)} %get-tuple-element.78), channel_id=1, source_target_pairs={{0,18},{2,16},{4,22},{6,20},{8,26},{10,24},{12,30},{14,28},{16,2},... | collective-permute-start | bytes 49160 | tf_op jit(solution)/shard_map/ppermute | solution.py:406
  10.2 0.0 collective-permute-done.13.f1
  10.2 6.2 %collective-permute-done.14.f2 = f32[2,16,128]{2,1,0:T(8,128)S(1)} collective-permute-done((f32[2,16,128]{2,1,0:T(8,128)S(1)}, f32[2,16,128]{2,1,0:T(8,128)S(1)}, u32[]{:S(2)}, u32[]{:S(2)}) %collective-permute-start.14) | collective-permute-done | bytes 16416 | tf_op jit(solution)/shard_map/ppermute | solution.py:406
  16.4 1.3 %collective-permute-done.15.f3 = f32[2,16,128]{2,1,0:T(8,128)S(1)} collective-permute-done((f32[2,16,128]{2,1,0:T(8,128)S(1)}, f32[2,16,128]{2,1,0:T(8,128)S(1)}, u32[]{:S(2)}, u32[]{:S(2)}) %collective-permute-start.15) | collective-permute-done | bytes 16416 | tf_op jit(solution)/shard_map/ppermute | solution.py:406
  17.7 0.2 shard_map.99
  17.9 1.3 %collective-permute-start.16 = (f32[2,64,128]{2,1,0:T(8,128)S(1)}, f32[2,64,128]{2,1,0:T(8,128)S(1)}, u32[]{:S(2)}, u32[]{:S(2)}) collective-permute-start(f32[2,64,128]{2,1,0:T(8,128)S(1)} %shard_map.99), channel_id=1, source_target_pairs={{0,4},{2,6},{4,0},{6,2},{8,12},{10,14},{12,8},{14,10},{16,20},{18,... | collective-permute-start | bytes 196616 | tf_op jit(solution)/shard_map/ppermute | solution.py:406
  19.2 1.9 %collective-permute-done.16 = f32[2,64,128]{2,1,0:T(8,128)S(1)} collective-permute-done((f32[2,64,128]{2,1,0:T(8,128)S(1)}, f32[2,64,128]{2,1,0:T(8,128)S(1)}, u32[]{:S(2)}, u32[]{:S(2)}) %collective-permute-start.16) | collective-permute-done | bytes 65568 | tf_op jit(solution)/shard_map/ppermute | solution.py:406
  21.1 2.6 %collective-permute-start.17 = (f32[2,64,128]{2,1,0:T(8,128)S(1)}, f32[2,64,128]{2,1,0:T(8,128)S(1)}, u32[]{:S(2)}, u32[]{:S(2)}) collective-permute-start(f32[2,64,128]{2,1,0:T(8,128)S(1)} %add.9), channel_id=1, source_target_pairs={{0,12},{2,14},{4,8},{6,10},{8,4},{10,6},{12,0},{14,2},{16,28},{18,... | collective-permute-start | bytes 196616 | tf_op jit(solution)/shard_map/ppermute | solution.py:406
  23.7 1.8 %collective-permute-done.17 = f32[2,64,128]{2,1,0:T(8,128)S(1)} collective-permute-done((f32[2,64,128]{2,1,0:T(8,128)S(1)}, f32[2,64,128]{2,1,0:T(8,128)S(1)}, u32[]{:S(2)}, u32[]{:S(2)}) %collective-permute-start.17) | collective-permute-done | bytes 65568 | tf_op jit(solution)/shard_map/ppermute | solution.py:406
  25.6 1.7 %collective-permute-start.18 = (f32[2,64,128]{2,1,0:T(8,128)S(1)}, f32[2,64,128]{2,1,0:T(8,128)S(1)}, u32[]{:S(2)}, u32[]{:S(2)}) collective-permute-start(f32[2,64,128]{2,1,0:T(8,128)S(1)} %add.10), channel_id=1, source_target_pairs={{0,32},{2,34},{4,36},{6,38},{8,40},{10,42},{12,44},{14,46},{16,48}... | collective-permute-start | bytes 196616 | tf_op jit(solution)/shard_map/ppermute | solution.py:406
  27.3 1.7 %collective-permute-done.18 = f32[2,64,128]{2,1,0:T(8,128)S(1)} collective-permute-done((f32[2,64,128]{2,1,0:T(8,128)S(1)}, f32[2,64,128]{2,1,0:T(8,128)S(1)}, u32[]{:S(2)}, u32[]{:S(2)}) %collective-permute-start.18) | collective-permute-done | bytes 65568 | tf_op jit(solution)/shard_map/ppermute | solution.py:406
  28.9 3.7 %collective-permute-start.19 = (f32[2,64,128]{2,1,0:T(8,128)S(1)}, f32[2,64,128]{2,1,0:T(8,128)S(1)}, u32[]{:S(2)}, u32[]{:S(2)}) collective-permute-start(f32[2,64,128]{2,1,0:T(8,128)S(1)} %add.11.m0), channel_id=1, source_target_pairs={{0,96},{2,98},{4,100},{6,102},{8,104},{10,106},{12,108},{14,110},{... | collective-permute-start | bytes 196616 | tf_op jit(solution)/shard_map/ppermute | solution.py:406
  33.3 9.2 %conditional.1 = (f32[45,8,128]{2,1,0:T(8,128)}, f32[45,8,128]{2,1,0:T(8,128)}) conditional(s32[]{:T(128)} %bitcast.2, (f32[45,8,128]{2,1,0:T(8,128)S(1)}, f32[45,8,128]{2,1,0:T(8,128)S(1)}) %tuple.29, (f32[45,8,128]{2,1,0:T(8,128)S(1)}, f32[45,8,128]{2,1,0:T(8,128)S(1)}) %tuple.29, (f32[45,8,128]{2,1,0:T(8,128)S(1)}, ...), branch_computations={%region_0.0_spmd, %region_1.0_spmd, %region_2.0_spmd, %region_3.0_... | conditional | bytes 1474656 | solution.py:480
  33.3 4.1 %collective-permute-start.8 = (f32[45,8,128]{2,1,0:T(8,128)S(1)}, f32[45,8,128]{2,1,0:T(8,128)}, u32[]{:S(2)}, u32[]{:S(2)}) collective-permute-start(f32[45,8,128]{2,1,0:T(8,128)S(1)} %get-tuple-element.37), channel_id=1, source_target_pairs={{0,2},{2,4},{4,6},{6,8},{8,10},{10,12},{12,14},{14,16},{16,18},{18... | collective-permute-start | bytes 552968 | tf_op jit(solution)/shard_map/cond/branch_4_fun/ppermute | solution.py:422
  37.4 0.2 collective-permute-start.9
  37.6 2.3 %collective-permute-done.8 = f32[45,8,128]{2,1,0:T(8,128)} collective-permute-done((f32[45,8,128]{2,1,0:T(8,128)S(1)}, f32[45,8,128]{2,1,0:T(8,128)}, u32[]{:S(2)}, u32[]{:S(2)}) %collective-permute-start.8) | collective-permute-done | bytes 184352 | tf_op jit(solution)/shard_map/cond/branch_4_fun/ppermute | solution.py:422
  39.9 2.6 %collective-permute-done.9 = f32[45,8,128]{2,1,0:T(8,128)} collective-permute-done((f32[45,8,128]{2,1,0:T(8,128)S(1)}, f32[45,8,128]{2,1,0:T(8,128)}, u32[]{:S(2)}, u32[]{:S(2)}) %collective-permute-start.9) | collective-permute-done | bytes 184352 | tf_op jit(solution)/shard_map/cond/branch_4_fun/ppermute | solution.py:422
  42.4 1.9 %shard_map.91 = (f32[45,240,128]{2,1,0:T(8,128)S(1)}, f32[128,64]{1,0:T(8,128)S(1)}, f32[128,128]{1,0:T(8,128)S(1)}, f32[97,8,128]{2,1,0:T(8,128)S(1)}) custom-call(s32[64]{0:T(128)} %rows_hbm.3, s32[2]{0:T(128)} %count_hbm.1, f32[3,3]{1,0:T(4,128)} %dis_hbm.1, f32[3]{0:T(128)} %freq_hbm.1, f32[3,5,3,5]{3,2,1,0:T(4,128)} %bitcast.12, f32[45,128,128]{2,1,0:T(8,128)} %bitcast.10), custom_call_target="tpu_custom_call" | custom-call | flops 3000000 | bytes 375000 | tf_op jit(solution)/shard_map/pallas_call | solution.py:487
  44.3 0.0 collective-permute-done.19.m1
  44.4 0.2 shard_map.100
  44.6 6.0 %collective-permute-start.20 = (f32[2,16,128]{2,1,0:T(8,128)S(1)}, f32[2,16,128]{2,1,0:T(8,128)S(1)}, u32[]{:S(2)}, u32[]{:S(2)}) collective-permute-start(f32[2,16,128]{2,1,0:T(8,128)S(1)} %get-tuple-element.82), channel_id=1, source_target_pairs={{0,2},{2,0},{4,6},{6,4},{8,10},{10,8},{12,14},{14,12},{16,18},{18,... | collective-permute-start | bytes 49160 | tf_op jit(solution)/shard_map/ppermute | solution.py:406
  50.7 0.0 collective-permute-start.21
  50.7 1.7 %collective-permute-start.22 = (f32[2,16,128]{2,1,0:T(8,128)S(1)}, f32[2,16,128]{2,1,0:T(8,128)S(1)}, u32[]{:S(2)}, u32[]{:S(2)}) collective-permute-start(f32[2,16,128]{2,1,0:T(8,128)S(1)} %get-tuple-element.84), channel_id=1, source_target_pairs={{0,18},{2,16},{4,22},{6,20},{8,26},{10,24},{12,30},{14,28},{16,2},... | collective-permute-start | bytes 49160 | tf_op jit(solution)/shard_map/ppermute | solution.py:406
  52.4 1.8 %shard_map.95 = (f32[45,128,128]{2,1,0:T(8,128)S(1)}, f32[45,128,128]{2,1,0:T(8,128)S(1)}) custom-call(f32[97,8,128]{2,1,0:T(8,128)S(1)} %get-tuple-element.64.coef, f32[45,240,128]{2,1,0:T(8,128)S(1)} %get-tuple-element.72.x_in.x, f32[45,128,128]{2,1,0:T(8,128)} %bitcast.11), custom_call_target="tpu_custom_call" | custom-call | flops 10000000 | bytes 1250000 | tf_op jit(solution)/shard_map/pallas_call | solution.py:503
  54.2 1.1 %shard_map.96.out_in = f32[45,128,128]{2,1,0:T(8,128)S(1)} custom-call(f32[97,8,128]{2,1,0:T(8,128)S(1)} %get-tuple-element.64.coef, f32[45,240,128]{2,1,0:T(8,128)S(1)} %get-tuple-element.72.x_in.x, f32[45,128,128]{2,1,0:T(8,128)S(1)} %get-tuple-element.74.refs_0_), custom_call_target="tpu_custom_call", output_to_operand_aliasing={{}: (2, {})} | custom-call | flops 9000000 | bytes 1125000 | tf_op jit(solution)/shard_map/pallas_call | solution.py:512
  55.3 0.0 collective-permute-done.12.edge
  55.3 0.0 copy-start
  55.3 1.2 %shard_map.94.x = f32[45,240,128]{2,1,0:T(8,128)S(1)} custom-call(f32[97,8,128]{2,1,0:T(8,128)S(1)} %get-tuple-element.64.coef, f32[45,8,128]{2,1,0:T(8,128)} %get-tuple-element.69.ghost_l, f32[45,8,128]{2,1,0:T(8,128)} %get-tuple-element.70.ghost_r, f32[45,16,128]{2,1,0:T(8,128)S(1)} %collective-permute-done.12.edge, ...), custom_call_target="tpu_custom_call", output_to_operand_aliasing={{}: (4, {})} | custom-call | flops 1000000 | bytes 125000 | tf_op jit(solution)/shard_map/pallas_call | solution.py:520
  56.5 0.0 copy-done
  56.5 0.9 %shard_map.97.out_in = f32[45,128,128]{2,1,0:T(8,128)S(1)} custom-call(f32[97,8,128]{2,1,0:T(8,128)S(1)} %get-tuple-element.64.coef, f32[45,240,128]{2,1,0:T(8,128)S(1)} %shard_map.94.x, f32[128,128]{1,0:T(8,128)S(1)} %bitcast.6, f32[45,128,128]{2,1,0:T(8,128)S(1)} %get-tuple-element.73.base, ...), custom_call_target="tpu_custom_call", output_to_operand_aliasing={{}: (4, {})} | custom-call | flops 10000000 | bytes 1250000 | tf_op jit(solution)/shard_map/pallas_call | solution.py:524
  57.4 2.5 %shard_map.98.acc = f32[45,128,128]{2,1,0:T(8,128)S(1)} custom-call(f32[97,8,128]{2,1,0:T(8,128)S(1)} %get-tuple-element.64.coef, f32[45,240,128]{2,1,0:T(8,128)S(1)} %shard_map.94.x, f32[128,128]{1,0:T(8,128)S(1)} %bitcast.7, f32[45,128,128]{2,1,0:T(8,128)S(1)} %get-tuple-element.73.base, ...), custom_call_target="tpu_custom_call", output_to_operand_aliasing={{}: (4, {})} | custom-call | flops 30000000 | bytes 3750000 | tf_op jit(solution)/shard_map/pallas_call | solution.py:524
  59.9 0.0 collective-permute-done.20.g1
  59.9 0.0 collective-permute-done.21.g2
  59.9 0.0 collective-permute-done.22.g3
  59.9 2.8 %shard_map.101 = f32[45,128,128]{2,1,0:T(8,128)} custom-call(f32[45,128,128]{2,1,0:T(8,128)S(1)} %shard_map.98.acc, f32[2,16,128]{2,1,0:T(8,128)S(1)} %get-tuple-element.81.g0, f32[2,16,128]{2,1,0:T(8,128)S(1)} %collective-permute-done.20.g1, f32[2,16,128]{2,1,0:T(8,128)S(1)} %collective-permute-done.21.g2, f32[2,16,128]{2,1,0:T(8,128)S(1)} %collective-permute-done.22.g3, ...), custom_call_target="tpu_custom_call" | custom-call | flops 10000000 | bytes 1250000 | tf_op jit(solution)/shard_map/pallas_call | solution.py:538
  (3 shorter events, 0.0 us)
Async XLA Ops:
  3.8 51.5 %collective-permute-start.12 = (f32[45,16,128]{2,1,0:T(8,128)S(1)}, f32[45,16,128]{2,1,0:T(8,128)S(1)}, u32[]{:S(2)}, u32[]{:S(2)}) collective-permute-start(f32[45,16,128]{2,1,0:T(8,128)S(1)} %get-tuple-element.71), channel_id=1, source_target_pairs={{0,1},{1,0},{2,3},{3,2},{4,5},{5,4},{6,7},{7,6},{8,9},{9,8},{10,11... | collective-permute-start | bytes 1105928 | tf_op jit(solution)/shard_map/ppermute | solution.py:476
  7.6 2.6 %collective-permute-start.13 = (f32[2,16,128]{2,1,0:T(8,128)S(1)}, f32[2,16,128]{2,1,0:T(8,128)S(1)}, u32[]{:S(2)}, u32[]{:S(2)}) collective-permute-start(f32[2,16,128]{2,1,0:T(8,128)S(1)} %get-tuple-element.76), channel_id=1, source_target_pairs={{0,2},{2,0},{4,6},{6,4},{8,10},{10,8},{12,14},{14,12},{16,18},{18,... | collective-permute-start | bytes 49160 | tf_op jit(solution)/shard_map/ppermute | solution.py:406
  8.6 7.8 %collective-permute-start.14 = (f32[2,16,128]{2,1,0:T(8,128)S(1)}, f32[2,16,128]{2,1,0:T(8,128)S(1)}, u32[]{:S(2)}, u32[]{:S(2)}) collective-permute-start(f32[2,16,128]{2,1,0:T(8,128)S(1)} %get-tuple-element.77), channel_id=1, source_target_pairs={{0,16},{2,18},{4,20},{6,22},{8,24},{10,26},{12,28},{14,30},{16,0},... | collective-permute-start | bytes 49160 | tf_op jit(solution)/shard_map/ppermute | solution.py:406
  9.0 8.7 %collective-permute-start.15 = (f32[2,16,128]{2,1,0:T(8,128)S(1)}, f32[2,16,128]{2,1,0:T(8,128)S(1)}, u32[]{:S(2)}, u32[]{:S(2)}) collective-permute-start(f32[2,16,128]{2,1,0:T(8,128)S(1)} %get-tuple-element.78), channel_id=1, source_target_pairs={{0,18},{2,16},{4,22},{6,20},{8,26},{10,24},{12,30},{14,28},{16,2},... | collective-permute-start | bytes 49160 | tf_op jit(solution)/shard_map/ppermute | solution.py:406
  17.9 3.2 %collective-permute-start.16 = (f32[2,64,128]{2,1,0:T(8,128)S(1)}, f32[2,64,128]{2,1,0:T(8,128)S(1)}, u32[]{:S(2)}, u32[]{:S(2)}) collective-permute-start(f32[2,64,128]{2,1,0:T(8,128)S(1)} %shard_map.99), channel_id=1, source_target_pairs={{0,4},{2,6},{4,0},{6,2},{8,12},{10,14},{12,8},{14,10},{16,20},{18,... | collective-permute-start | bytes 196616 | tf_op jit(solution)/shard_map/ppermute | solution.py:406
  21.1 4.4 %collective-permute-start.17 = (f32[2,64,128]{2,1,0:T(8,128)S(1)}, f32[2,64,128]{2,1,0:T(8,128)S(1)}, u32[]{:S(2)}, u32[]{:S(2)}) collective-permute-start(f32[2,64,128]{2,1,0:T(8,128)S(1)} %add.9), channel_id=1, source_target_pairs={{0,12},{2,14},{4,8},{6,10},{8,4},{10,6},{12,0},{14,2},{16,28},{18,... | collective-permute-start | bytes 196616 | tf_op jit(solution)/shard_map/ppermute | solution.py:406
  25.6 3.4 %collective-permute-start.18 = (f32[2,64,128]{2,1,0:T(8,128)S(1)}, f32[2,64,128]{2,1,0:T(8,128)S(1)}, u32[]{:S(2)}, u32[]{:S(2)}) collective-permute-start(f32[2,64,128]{2,1,0:T(8,128)S(1)} %add.10), channel_id=1, source_target_pairs={{0,32},{2,34},{4,36},{6,38},{8,40},{10,42},{12,44},{14,46},{16,48}... | collective-permute-start | bytes 196616 | tf_op jit(solution)/shard_map/ppermute | solution.py:406
  28.9 15.4 %collective-permute-start.19 = (f32[2,64,128]{2,1,0:T(8,128)S(1)}, f32[2,64,128]{2,1,0:T(8,128)S(1)}, u32[]{:S(2)}, u32[]{:S(2)}) collective-permute-start(f32[2,64,128]{2,1,0:T(8,128)S(1)} %add.11.m0), channel_id=1, source_target_pairs={{0,96},{2,98},{4,100},{6,102},{8,104},{10,106},{12,108},{14,110},{... | collective-permute-start | bytes 196616 | tf_op jit(solution)/shard_map/ppermute | solution.py:406
  33.3 6.6 %collective-permute-start.8 = (f32[45,8,128]{2,1,0:T(8,128)S(1)}, f32[45,8,128]{2,1,0:T(8,128)}, u32[]{:S(2)}, u32[]{:S(2)}) collective-permute-start(f32[45,8,128]{2,1,0:T(8,128)S(1)} %get-tuple-element.37), channel_id=1, source_target_pairs={{0,2},{2,4},{4,6},{6,8},{8,10},{10,12},{12,14},{14,16},{16,18},{18... | collective-permute-start | bytes 552968 | tf_op jit(solution)/shard_map/cond/branch_4_fun/ppermute | solution.py:422
  37.4 5.1 %collective-permute-start.9 = (f32[45,8,128]{2,1,0:T(8,128)S(1)}, f32[45,8,128]{2,1,0:T(8,128)}, u32[]{:S(2)}, u32[]{:S(2)}) collective-permute-start(f32[45,8,128]{2,1,0:T(8,128)S(1)} %get-tuple-element.38), channel_id=1, source_target_pairs={{2,0},{4,2},{6,4},{8,6},{10,8},{12,10},{14,12},{16,14},{18,16},{20... | collective-permute-start | bytes 552968 | tf_op jit(solution)/shard_map/cond/branch_4_fun/ppermute | solution.py:422
  44.6 15.3 %collective-permute-start.20 = (f32[2,16,128]{2,1,0:T(8,128)S(1)}, f32[2,16,128]{2,1,0:T(8,128)S(1)}, u32[]{:S(2)}, u32[]{:S(2)}) collective-permute-start(f32[2,16,128]{2,1,0:T(8,128)S(1)} %get-tuple-element.82), channel_id=1, source_target_pairs={{0,2},{2,0},{4,6},{6,4},{8,10},{10,8},{12,14},{14,12},{16,18},{18,... | collective-permute-start | bytes 49160 | tf_op jit(solution)/shard_map/ppermute | solution.py:406
  50.7 9.3 %collective-permute-start.21 = (f32[2,16,128]{2,1,0:T(8,128)S(1)}, f32[2,16,128]{2,1,0:T(8,128)S(1)}, u32[]{:S(2)}, u32[]{:S(2)}) collective-permute-start(f32[2,16,128]{2,1,0:T(8,128)S(1)} %get-tuple-element.83), channel_id=1, source_target_pairs={{0,16},{2,18},{4,20},{6,22},{8,24},{10,26},{12,28},{14,30},{16,0},... | collective-permute-start | bytes 49160 | tf_op jit(solution)/shard_map/ppermute | solution.py:406
  50.7 9.3 %collective-permute-start.22 = (f32[2,16,128]{2,1,0:T(8,128)S(1)}, f32[2,16,128]{2,1,0:T(8,128)S(1)}, u32[]{:S(2)}, u32[]{:S(2)}) collective-permute-start(f32[2,16,128]{2,1,0:T(8,128)S(1)} %get-tuple-element.84), channel_id=1, source_target_pairs={{0,18},{2,16},{4,22},{6,20},{8,26},{10,24},{12,30},{14,28},{16,2},... | collective-permute-start | bytes 49160 | tf_op jit(solution)/shard_map/ppermute | solution.py:406
  55.3 1.2 %copy-start = (f32[8,16,128]{2,1,0:T(8,128)S(1)}, f32[8,16,128]{2,1,0:T(8,128)}, u32[]{:S(2)}) copy-start(f32[8,16,128]{2,1,0:T(8,128)} %param.17) | copy-start | bytes 196612
where the time goes:
time: 63 us; the launch traced here: 62.8 us
  starting transfers between devices  27.7 us (44%)
  waiting for transfers between devices  17.8 us (28%)
  Pallas kernels  16.5 us (26%)
  between operations  0.79 us (1%)
    ppermute x10, starting transfers between devices, swap(): return lax.ppermute(x, BLK, [(i, i ^ mask) for i in range(64)])  19.6 us
    ppermute x10, waiting for transfers between devices, swap(): return lax.ppermute(x, BLK, [(i, i ^ mask) for i in range(64)])  12.9 us
    ppermute x2, waiting for transfers between devices, run(): return (lax.ppermute(rim_r, BLK, right), lax.ppermute(rim_l, BLK, left))  4.87 us
    ppermute x2, starting transfers between devices, run(): return (lax.ppermute(rim_r, BLK, right), lax.ppermute(rim_l, BLK, left))  4.29 us
    ppermute x1, starting transfers between devices, per_device(): from_span = lax.ppermute(edge, 'span', [(0, 1), (1, 0)])  3.81 us
    pallas_call x2, Pallas kernels, per_device(): call(functools.partial(across_kernel, first, last), whole, [vspec()] * 5,...  3.39 us
    pallas_call x1, Pallas kernels, per_device(): call(finish_kernel, sds(45, 128, 128), [vspec()] * 8, hspec(), [VMEM((45,...  2.85 us
    pallas_call x1, Pallas kernels, per_device(): call(faces_kernel, [quarter] * 4 + [sds(8, 16, 128), padded], [hspec()],...  2.37 us
  transfers between devices with their start and end apart: 13, of which 7 were waited for; matrix products, arithmetic and copies ran while one was open for 0% of the time, Pallas kernels for 16%

commit v1 on v0

--- a/solution.py
+++ b/solution.py
@@ -10,26 +10,25 @@
 from jax.sharding import PartitionSpec as P
 
 BLK = ("blk_0", "blk_1", "blk_2", "blk_3")
-ORDERS = ((2, 33, 29), (2, 29, 33), (33, 2, 29), (33, 29, 2), (29, 2, 33), (29, 33, 2))
+ENDS = (
+    ((0, 32), (2, 34), (31, 63), (29, 61)),
+    ((0, 28), (2, 30), (35, 63), (33, 61)),
+)
 EXACT = lax.Precision.HIGHEST
 VMEM = pltpu.VMEM
 F32 = jnp.float32
 QUAD = (0, 1, 8, 9)
-HOPS = (2, 6, 16, 48)
+HOPS = (16, 48, 2, 6)
 DN = tuple(0.5 * math.cos(math.pi * n) / math.sin(math.pi * n / 9) for n in range(5) if n)
 
 
 ALONG = ((0, 5), (5, 8))
-ACROSS = ((0, 2), (2, 8))
-CENTRE, WAVE, SPAN, COEFS = 90, 91, 95, 97
+ACROSS = ((0, 1), (1, 5), (5, 8))
+CENTRE, WAVE, SPAN, LEFT, RIGHT, COEFS = 90, 91, 95, 97, 98, 99
 
 
 def vspec():
     return pl.BlockSpec(memory_space=VMEM)
-
-
-def sspec():
-    return pl.BlockSpec(memory_space=pltpu.SMEM)
 
 
 def hspec():
@@ -116,8 +115,8 @@
     return [place_in_row(order, lax.bitwise_xor(block, m)) for m in QUAD]
 
 
-def write_forward(members, forward):
-    its_row, _, mode, period, cos, sin = waves(members)
+def write_forward(its_waves, forward):
+    its_row, _, mode, period, cos, sin = its_waves
     weight = jnp.where(mode == 0, 2.0, 4.0) / period
     for r in range(3):
         here = its_row == r
@@ -125,9 +124,14 @@
         forward[pl.ds(32 * r + 16, 16), :] = jnp.where(here, sin * weight, 0.0)[:, :64]
 
 
-def write_rest(members, count, dis, freq, jac, backward, mixing, coef):
-    row = members[0][0]
-    its_row, lane, mode, _, cos, sin = waves(members)
+def write_rest(block, members, its_waves, count, dis, freq, jac, backward, mixing, coef):
+    row, position, total = members[0]
+    far_end = jnp.where(total == 33, 2.0, 3.0)
+    even = (block & 1) == 0
+    to_next, to_last = jnp.where(even, 0.0, 1.0), jnp.where(even, 1.0, 0.0)
+    before = jnp.where(position > 0, to_last, jnp.where(total == 2, to_next, far_end))
+    after = jnp.where(position < total - 1, to_next, jnp.where(total == 2, to_last, far_end))
+    its_row, lane, mode, _, cos, sin = its_waves
     seen = its_row - jnp.where(lane < 64, 1, 0)
     back = []
     for gap in range(2):
@@ -173,11 +177,13 @@
     for n in range(4):
         put(WAVE + n, freq[row] * DN[n])
     upper = lax.axis_index("span")
+    put(LEFT, before)
+    put(RIGHT, after)
     put(SPAN, upper.astype(F32))
     put(SPAN + 1, (1 - upper).astype(F32))
 
 
-def faces_kernel(x_hbm, f0, f1, f2, f3, faces, x, sem):
+def faces_kernel(x_hbm, kept, sent, faces, x, sem):
     copies = [
         pltpu.make_async_copy(
             x_hbm.at[:, pl.ds(16 * s, 16), :], x.at[:, pl.ds(24 * s + 32, 16), :], sem.at[s]
@@ -196,94 +202,93 @@
                 acc[h] = jnp.where(lane == j, turned, acc[h])
         for h in range(2):
             faces[s, pl.ds(8 * h, 8), :] = acc[h]
-    q = own_quarter()
-    for d, ref in enumerate((f0, f1, f2, f3)):
-        ref[...] = faces[pl.ds(2 * lax.bitwise_xor(q, d), 2)]
+    core = lax.axis_index("blk_3")
+    for y in range(2):
+        kept[y] = faces[pl.ds(4 * y + 2 * core, 2)]
+        sent[y] = faces[pl.ds(4 * y + 2 - 2 * core, 2)]
+
+
+def pair_kernel(kept, other, sent):
+    y = 1 - lax.axis_index("blk_1")
+    sent[0] = kept[y]
+    sent[1] = other[y]
+
+
+def pack_kernel(first, second, sent):
+    sent[0] = first[...]
+    sent[1] = second[1]
 
 
 def leave_kernel(
-    rows_hbm, lag_hbm, x, order_ref, rim_l, rim_r, edge, forward, rows, lag, sem
-):
-    small = [
-        pltpu.make_async_copy(a, b, sem.at[n])
-        for n, (a, b) in enumerate(((rows_hbm, rows), (lag_hbm, lag)))
-    ]
-    for copy in small:
-        copy.start()
-    outer = pl.multiple_of(jnp.where(lax.axis_index("span") == 0, 200, 32), 8)
-
-    @pl.loop(0, 9)
-    def _(k):
-        for v in range(5):
-            edge[v * 9 + k] = x[v * 9 + k, pl.ds(outer, 16), :]
-
-    for copy in small:
-        copy.wait()
-    order = order_of(rows)
-    order_ref[0] = order
-    members = members_of(order)
-    write_forward(members, forward)
-    row, position, total = members[0]
-    turn_left = jnp.where(position == 0, 9 - lag[row], 0)
-    turn_right = jnp.where(position == total - 1, lag[row], 0)
-
-    @pl.loop(0, 9)
-    def _(k):
-        for v in range(5):
-            j = v * 9 + k
-            rim_l[j] = x[v * 9 + lax.rem(k + turn_left, 9), pl.ds(32, 8, stride=24), :]
-            rim_r[j] = x[v * 9 + lax.rem(k + turn_right, 9), pl.ds(47, 8, stride=24), :]
-
-
-def tables_kernel(
-    rows_hbm, count_hbm, dis_hbm, freq_hbm, jac_hbm, x_hbm,
-    x, backward, mixing, coef, rows, count, dis, freq, jac, sem, sem_x,
+    rows_hbm, lag_hbm, count_hbm, dis_hbm, freq_hbm, jac_hbm, dt_hbm, x,
+    rims, rim_w, edge, forward, backward, mixing, coef, dt,
+    rows, lag, count, dis, freq, jac, sem,
 ):
     small = [
         pltpu.make_async_copy(a, b, sem.at[n])
         for n, (a, b) in enumerate(
             (
-                (rows_hbm, rows), (count_hbm, count),
-                (dis_hbm, dis), (freq_hbm, freq), (jac_hbm, jac),
+                (rows_hbm, rows), (lag_hbm, lag), (count_hbm, count),
+                (dis_hbm, dis), (freq_hbm, freq), (jac_hbm, jac), (dt_hbm, dt),
             )
         )
     ]
-    copies = [
-        pltpu.make_async_copy(
-            x_hbm.at[:, pl.ds(16 * s, 16), :], x.at[:, pl.ds(24 * s + 32, 16), :], sem_x.at[s]
-        )
-        for s in range(8)
-    ]
-    for copy in small + copies:
+    for copy in small:
         copy.start()
+    outer = pl.multiple_of(jnp.where(lax.axis_index("span") == 0, 200, 32), 8)
+
+    @pl.loop(0, 9)
+    def _(k):
+        for v in range(5):
+            edge[v * 9 + k] = x[v * 9 + k, pl.ds(outer, 16), :]
+
     for copy in small:
         copy.wait()
-    write_rest(members_of(order_of(rows)), count, dis, freq, jac, backward, mixing, coef)
-    for copy in copies:
-        copy.wait()
-
-
-def project_kernel(f0, f1, f2, f3, forward, out):
+    members = members_of(order_of(rows))
+    its_waves = waves(members)
+    write_forward(its_waves, forward)
+    write_rest(own_block(), members, its_waves, count, dis, freq, jac, backward, mixing, coef)
+    row, position, total = members[0]
+    at_begin, at_final = position == 0, position == total - 1
+    turn = jnp.where(at_begin, 9 - lag[row], lag[row])
+    end = jnp.where(at_begin, 32, 47)
+    turn_left = jnp.where(at_begin & (total == 2), turn, 0)
+    turn_right = jnp.where(at_final & (total == 2), turn, 0)
+
+    @pl.loop(0, 9)
+    def _(k):
+        for v in range(5):
+            j = v * 9 + k
+            rims[j] = x[v * 9 + lax.rem(k + turn_left, 9), pl.ds(32, 8, stride=24), :]
+            rims[45 + j] = x[v * 9 + lax.rem(k + turn_right, 9), pl.ds(47, 8, stride=24), :]
+            rim_w[j] = x[v * 9 + lax.rem(k + turn, 9), pl.ds(end, 8, stride=24), :]
+
+
+def project_kernel(kept, other, far, forward, out):
+    y = lax.axis_index("blk_1")
     even = lax.broadcasted_iota(jnp.int32, (32, 128), 1) % 2 == 0
     for i in range(2):
-        columns = jnp.concatenate([f0[i], f1[i], f2[i], f3[i]], axis=0)
+        columns = jnp.concatenate([kept[y, i], other[y, i], far[0, i], far[1, i]], axis=0)
         parts = jnp.dot(forward[...], columns, precision=EXACT, preferred_element_type=F32)
         low, mid, high = parts[:32], parts[32:64], parts[64:]
         out[i, pl.ds(0, 32), :] = jnp.where(even, low, mid)
         out[i, pl.ds(32, 32), :] = jnp.where(even, mid, high)
 
 
-def evaluate_kernel(m0, m1, backward, g0, g1, g2, g3):
+def evaluate_kernel(m0, m1, backward, own, core, far):
     even = lax.broadcasted_iota(jnp.int32, (64, 128), 1) % 2 == 0
     for i in range(2):
         modes = m0[i] + m1[i]
         both = jnp.dot(backward[...], modes, precision=EXACT, preferred_element_type=F32)
         ghost = jnp.where(even, both[:64], both[64:])
-        for d, ref in enumerate((g0, g1, g2, g3)):
-            ref[i] = ghost[16 * d : 16 * d + 16]
-
-
-def ghosts_kernel(coef, ghost_l, ghost_r, edge, x_in, x):
+        own[i] = ghost[:16]
+        core[i] = ghost[16:32]
+        far[0, i] = ghost[32:48]
+        far[1, i] = ghost[48:]
+
+
+def ghosts_kernel(coef, core, chip, wrap0, wrap1, edge, x_in, x):
+    left, right = coef[LEFT], coef[RIGHT]
     keep_low = jnp.concatenate([coef[SPAN]] * 2, axis=0)
     keep_high = jnp.concatenate([coef[SPAN + 1]] * 2, axis=0)
 
@@ -291,8 +296,14 @@
     def _(k):
         for v in range(5):
             j = v * 9 + k
-            x[j, pl.ds(31, 8, stride=24), :] = ghost_l[j]
-            x[j, pl.ds(48, 8, stride=24), :] = ghost_r[j]
+            low, high = core[45 + j], core[j]
+            low = jnp.where(left == 1, chip[45 + j], low)
+            high = jnp.where(right == 1, chip[j], high)
+            for w, wrap in ((2, wrap0), (3, wrap1)):
+                low = jnp.where(left == w, wrap[j], low)
+                high = jnp.where(right == w, wrap[j], high)
+            x[j, pl.ds(31, 8, stride=24), :] = low
+            x[j, pl.ds(48, 8, stride=24), :] = high
             x[j, pl.ds(8, 16), :] = edge[j] * keep_low
             x[j, pl.ds(224, 16), :] = edge[j] * keep_high
 
@@ -377,9 +388,9 @@
                     out[u * 9 + k, there, :] = acc[u] + part
 
 
-def finish_kernel(acc, g0, g1, g2, g3, faces, mixing, dt, out_hbm, out, ghost, sem):
+def finish_kernel(acc, own, core, far, faces, mixing, dt, out_hbm, out, ghost, sem):
     q = own_quarter()
-    for d, ref in enumerate((g0, g1, g2, g3)):
+    for d, ref in enumerate((own, core.at[0], far.at[0], core.at[1])):
         for i in range(2):
             s = 2 * lax.bitwise_xor(q, d) + i
             ghost[pl.ds(pl.multiple_of(16 * s, 16), 16), :] = ref[i] - faces[s]
@@ -406,22 +417,9 @@
     return lax.ppermute(x, BLK, [(i, i ^ mask) for i in range(64)])
 
 
-def ring(order):
-    pairs, begin = [], 0
-    for length in order:
-        pairs += [(begin + i, begin + (i + 1) % length) for i in range(length)]
-        begin += length
-    return pairs
-
-
-def ring_swaps(order):
-    right = ring(order)
-    left = [(t, s) for s, t in right]
-
-    def run(rim_l, rim_r):
-        return lax.ppermute(rim_r, BLK, right), lax.ppermute(rim_l, BLK, left)
-
-    return run
+def other_end(x, pairs):
+    ends = dict(pairs) | {b: a for a, b in pairs}
+    return lax.ppermute(x, BLK, [(i, ends.get(i, i)) for i in range(64)])
 
 
 def sds(*shape, dtype=F32):
@@ -447,59 +445,50 @@
     b = base.reshape(45, 128, 128)
     dt = dt.reshape(128, 128)
     jac = jac.transpose(0, 2, 1, 3)
-    x, b, row_map, lag, count, dis, freq, jac = [
+    x, b, dt, row_map, lag, count, dis, freq, jac = [
         pltpu.with_memory_space_constraint(a, pltpu.HBM)
-        for a in (x, b, row_map, lag, count, dis, freq, jac)
+        for a in (x, b, dt, row_map, lag, count, dis, freq, jac)
     ]
     quarter, rim = sds(2, 16, 128), sds(45, 8, 128)
     padded, whole = VMEM((45, 240, 128), F32), VMEM((45, 128, 128), F32)
     dma = pltpu.SemaphoreType.DMA
-    x_hbm = x
-    f0, f1, f2, f3, faces, x = call(
-        faces_kernel,
-        [quarter] * 4 + [sds(8, 16, 128), padded],
-        [hspec()],
-        [vspec()] * 6,
-        [dma((8,))],
+    pair = sds(2, 2, 16, 128)
+    kept, sent, faces, x = call(
+        faces_kernel, [pair, pair, sds(8, 16, 128), padded], [hspec()], [vspec()] * 4, [dma((8,))]
     )(x)
-    r = []
-    for d, f in ((1, f1), (2, f2), (3, f3)):
-        r.append(swap(f, QUAD[d]))
-    order, rim_l, rim_r, edge, forward = call(
+    other = swap(sent, 1)
+    sent = call(pair_kernel, pair, [vspec()] * 2, vspec())(kept, other)
+    far = swap(sent, 8)
+    rims, rim_w, edge, forward, backward, mixing, coef, dt = call(
         leave_kernel,
-        [sds(1, dtype=jnp.int32), rim, rim, sds(45, 16, 128), sds(96, 64)],
-        [hspec()] * 2 + [vspec()],
-        [sspec()] + [vspec()] * 4,
-        [pltpu.SMEM((64,), jnp.int32), pltpu.SMEM((3,), jnp.int32), dma((2,))],
+        [sds(90, 8, 128), rim, sds(45, 16, 128), sds(96, 64)]
+        + [sds(128, 64), sds(128, 128), sds(COEFS, 8, 128), sds(128, 128)],
+        [hspec()] * 7 + [vspec()],
+        [vspec()] * 8,
+        [
+            pltpu.SMEM((64,), jnp.int32),
+            pltpu.SMEM((3,), jnp.int32),
+            pltpu.SMEM((2,), jnp.int32),
+            pltpu.SMEM((3, 3), F32),
+            pltpu.SMEM((3,), F32),
+            pltpu.SMEM((3, 5, 3, 5), F32),
+            dma((7,)),
+        ],
         flops=2000000,
-    )(row_map, lag, x)
+    )(row_map, lag, count, dis, freq, jac, dt, x)
     from_span = lax.ppermute(edge, "span", [(0, 1), (1, 0)])
     modes = call(
-        project_kernel, sds(2, 64, 128), [vspec()] * 5, vspec(), flops=1000000
-    )(f0, *r, forward)
-    from_left, from_right = lax.switch(
-        order[0], [ring_swaps(lengths) for lengths in ORDERS], rim_l, rim_r
-    )
+        project_kernel, sds(2, 64, 128), [vspec()] * 4, vspec(), flops=1000000
+    )(kept, other, far, forward)
+    from_core = swap(rims, 1)
+    from_chip = other_end(rims, [(i, i + 1) for i in range(1, 63, 2)])
+    wraps = []
+    for pairs in ENDS:
+        wraps.append(other_end(rim_w, pairs))
     for n, mask in enumerate(HOPS):
         other = swap(modes, mask)
         if n < 3:
             modes = modes + other
-    x, backward, mixing, coef = call(
-        tables_kernel,
-        [padded, sds(128, 64), sds(128, 128), sds(COEFS, 8, 128)],
-        [hspec()] * 6,
-        [vspec()] * 4,
-        [
-            pltpu.SMEM((64,), jnp.int32),
-            pltpu.SMEM((2,), jnp.int32),
-            pltpu.SMEM((3, 3), F32),
-            pltpu.SMEM((3,), F32),
-            pltpu.SMEM((3, 5, 3, 5), F32),
-            dma((5,)),
-            dma((8,)),
-        ],
-        flops=3000000,
-    )(row_map, count, dis, freq, jac, x_hbm)
     acc, b = call(
         functools.partial(along_first_kernel, *ALONG[0]),
         [whole, whole],
@@ -518,8 +507,8 @@
             aliases={2: 0},
         )(coef, x, acc)
     x = call(
-        ghosts_kernel, padded, [vspec()] * 5, vspec(), flops=1000000, aliases={4: 0}
-    )(coef, from_left, from_right, from_span, x)
+        ghosts_kernel, padded, [vspec()] * 7, vspec(), flops=1000000, aliases={6: 0}
+    )(coef, from_core, from_chip, *wraps, from_span, x)
     for first, last in ACROSS:
         acc = call(
             functools.partial(across_kernel, first, last),
@@ -529,20 +518,20 @@
             flops=5000000 * (last - first),
             aliases={4: 0},
         )(coef, x, dt, b, acc)
-    g = call(
-        evaluate_kernel, [quarter] * 4, [vspec()] * 3, [vspec()] * 4, flops=1000000
+    own, core, far = call(
+        evaluate_kernel, [quarter, quarter, pair], [vspec()] * 3, [vspec()] * 3, flops=1000000
     )(modes, other, backward)
-    h = []
-    for d in (1, 2, 3):
-        h.append(swap(g[d], QUAD[d]))
+    far = swap(far, 8)
+    core = call(pack_kernel, pair, [vspec()] * 2, vspec())(core, far)
+    core = swap(core, 1)
     out = call(
         finish_kernel,
         sds(45, 128, 128),
-        [vspec()] * 8,
+        [vspec()] * 7,
         hspec(),
         [VMEM((45, 128, 128), F32), VMEM((128, 128), F32), dma((5,))],
         flops=10000000,
-    )(acc, g[0], *h, faces, mixing, dt)
+    )(acc, own, core, far, faces, mixing, dt)
     return out.reshape(shape)
 
 

time: 63 us -> 58.2 us (0.924)
  waiting for transfers between devices: 17.8 us -> 10 us
  starting transfers between devices: 27.7 us -> 34 us
  Pallas kernels: 16.5 us -> 13.7 us
    ppermute x2 -> x3, waiting for transfers between devices: 4.87 us -> 0.01 us  [other_end(): return lax.ppermute(x, BLK, [(i, ends.get(i, i)) for i in range(64)])]
    ppermute x10 -> x9, starting transfers between devices: 19.6 us -> 23.7 us  [swap(): return lax.ppermute(x, BLK, [(i, i ^ mask) for i in range(64)])]
    ppermute x2 -> x3, starting transfers between devices: 4.29 us -> 7.52 us  [other_end(): return lax.ppermute(x, BLK, [(i, ends.get(i, i)) for i in range(64)])]
    ppermute x10 -> x9, waiting for transfers between devices: 12.9 us -> 10 us  [swap(): return lax.ppermute(x, BLK, [(i, i ^ mask) for i in range(64)])]
    pallas_call x7 -> x8, Pallas kernels: 10.2 us -> 7.47 us  [the longest x1 2.85 us: per_device(): call(finish_kernel, sds(45, 128, 128), [vspec()] * 7, hspec(), [VMEM((45,...]
    ppermute x1, starting transfers between devices: 3.81 us -> 2.77 us  [per_device(): from_span = lax.ppermute(edge, 'span', [(0, 1), (1, 0)])]
    pallas_call x2 -> x3, Pallas kernels: 3.39 us -> 3.32 us  [per_device(): call(functools.partial(across_kernel, first, last), whole, [vspec()] * 5,...]
  transfers between devices with their start and end apart: 13 -> 13, of which waited for: 7 -> 5; matrix products, arithmetic and copies ran while one was open for 0% -> 0% of each run, Pallas kernels for 16% -> 14%
where the time goes in v1:
time: 58.2 us; the launch traced here: 57.9 us
  starting transfers between devices  34 us (58%)
  Pallas kernels  13.7 us (24%)
  waiting for transfers between devices  10 us (17%)
    ppermute x9, starting transfers between devices, swap(): return lax.ppermute(x, BLK, [(i, i ^ mask) for i in range(64)])  23.7 us
    ppermute x9, waiting for transfers between devices, swap(): return lax.ppermute(x, BLK, [(i, i ^ mask) for i in range(64)])  10 us
    ppermute x3, starting transfers between devices, other_end(): return lax.ppermute(x, BLK, [(i, ends.get(i, i)) for i in range(64)])  7.52 us
    pallas_call x3, Pallas kernels, per_device(): call(functools.partial(across_kernel, first, last), whole, [vspec()] * 5,...  3.32 us
    pallas_call x1, Pallas kernels, per_device(): call(finish_kernel, sds(45, 128, 128), [vspec()] * 7, hspec(), [VMEM((45,...  2.85 us
    ppermute x1, starting transfers between devices, per_device(): from_span = lax.ppermute(edge, 'span', [(0, 1), (1, 0)])  2.77 us
    pallas_call x1, Pallas kernels, per_device(): call(faces_kernel, [pair, pair, sds(8, 16, 128), padded], [hspec()], [vsp...  2.37 us
    pallas_call x1, Pallas kernels, per_device(): call(functools.partial(along_first_kernel, *ALONG[0]), [whole, whole], [v...  1.84 us
  transfers between devices with their start and end apart: 13, of which 5 were waited for; matrix products, arithmetic and copies ran while one was open for 0% of the time, Pallas kernels for 14%

profile of v1, /device:TPU:1, one launch (start us, length us, event | category | flops | bytes accessed | tf_op | source)
XLA Modules:
  0.0 57.9 jit_solution(14941400735140471485)
XLA Ops:
  0.0 2.4 %shard_map.91 = (f32[2,2,16,128]{3,2,1,0:T(8,128)S(1)}, f32[2,2,16,128]{3,2,1,0:T(8,128)S(1)}, f32[8,16,128]{2,1,0:T(8,128)S(1)}, f32[45,240,128]{2,1,0:T(8,128)S(1)}) custom-call(f32[45,128,128]{2,1,0:T(8,128)} %bitcast.5), custom_call_target="tpu_custom_call" | custom-call | tf_op jit(solution)/shard_map/pallas_call | solution.py:456
  2.4 1.5 %collective-permute-start.5 = (f32[2,2,16,128]{3,2,1,0:T(8,128)S(1)}, f32[2,2,16,128]{3,2,1,0:T(8,128)S(1)}, u32[]{:S(2)}, u32[]{:S(2)}) collective-permute-start(f32[2,2,16,128]{3,2,1,0:T(8,128)S(1)} %get-tuple-element.31), channel_id=1, source_target_pairs={{0,2},{2,0},{4,6},{6,4},{8,10},{10,8},{12,14},{14,12},{16,18},{18,... | collective-permute-start | bytes 98312 | tf_op jit(solution)/shard_map/ppermute | solution.py:417
  3.8 0.9 %collective-permute-done.5.other = f32[2,2,16,128]{3,2,1,0:T(8,128)S(1)} collective-permute-done((f32[2,2,16,128]{3,2,1,0:T(8,128)S(1)}, f32[2,2,16,128]{3,2,1,0:T(8,128)S(1)}, u32[]{:S(2)}, u32[]{:S(2)}) %collective-permute-start.5) | collective-permute-done | bytes 32800 | tf_op jit(solution)/shard_map/ppermute | solution.py:417
  4.7 1.4 %collective-permute-start.6 = (f32[2,2,16,128]{3,2,1,0:T(8,128)S(1)}, f32[2,2,16,128]{3,2,1,0:T(8,128)S(1)}, u32[]{:S(2)}, u32[]{:S(2)}) collective-permute-start(f32[2,2,16,128]{3,2,1,0:T(8,128)S(1)} %shard_map.99), channel_id=1, source_target_pairs={{0,16},{2,18},{4,20},{6,22},{8,24},{10,26},{12,28},{14,30},{16,0},... | collective-permute-start | bytes 98312 | tf_op jit(solution)/shard_map/ppermute | solution.py:417
  6.1 1.6 %shard_map.92 = (f32[90,8,128]{2,1,0:T(8,128)S(1)}, f32[45,8,128]{2,1,0:T(8,128)S(1)}, f32[45,16,128]{2,1,0:T(8,128)S(1)}, f32[96,64]{1,0:T(8,128)S(1)}, f32[128...) custom-call(s32[64]{0:T(128)} %rows_hbm.1, s32[3]{0:T(128)} %lag_hbm.1, ...), custom_call_target="tpu_custom_call" | custom-call | flops 2000000 | bytes 250000 | tf_op jit(solution)/shard_map/pallas_call | solution.py:462
  7.7 0.0 collective-permute-done.6.far
  7.7 0.2 shard_map.100
  8.0 1.7 %collective-permute-start.7 = (f32[2,64,128]{2,1,0:T(8,128)S(1)}, f32[2,64,128]{2,1,0:T(8,128)S(1)}, u32[]{:S(2)}, u32[]{:S(2)}) collective-permute-start(f32[2,64,128]{2,1,0:T(8,128)S(1)} %shard_map.100), channel_id=1, source_target_pairs={{0,32},{2,34},{4,36},{6,38},{8,40},{10,42},{12,44},{14,46},{16,48}... | collective-permute-start | bytes 196616 | tf_op jit(solution)/shard_map/ppermute | solution.py:417
  9.7 1.7 %collective-permute-done.7 = f32[2,64,128]{2,1,0:T(8,128)S(1)} collective-permute-done((f32[2,64,128]{2,1,0:T(8,128)S(1)}, f32[2,64,128]{2,1,0:T(8,128)S(1)}, u32[]{:S(2)}, u32[]{:S(2)}) %collective-permute-start.7) | collective-permute-done | bytes 65568 | tf_op jit(solution)/shard_map/ppermute | solution.py:417
  11.3 3.7 %collective-permute-start.8 = (f32[2,64,128]{2,1,0:T(8,128)S(1)}, f32[2,64,128]{2,1,0:T(8,128)S(1)}, u32[]{:S(2)}, u32[]{:S(2)}) collective-permute-start(f32[2,64,128]{2,1,0:T(8,128)S(1)} %add.9), channel_id=1, source_target_pairs={{0,96},{2,98},{4,100},{6,102},{8,104},{10,106},{12,108},{14,110},{... | collective-permute-start | bytes 196616 | tf_op jit(solution)/shard_map/ppermute | solution.py:417
  15.0 2.8 %collective-permute-start.4 = (f32[45,16,128]{2,1,0:T(8,128)S(1)}, f32[45,16,128]{2,1,0:T(8,128)S(1)}, u32[]{:S(2)}, u32[]{:S(2)}) collective-permute-start(f32[45,16,128]{2,1,0:T(8,128)S(1)} %get-tuple-element.26), channel_id=1, source_target_pairs={{0,1},{1,0},{2,3},{3,2},{4,5},{5,4},{6,7},{7,6},{8,9},{9,8},{10,11... | collective-permute-start | bytes 1105928 | tf_op jit(solution)/shard_map/ppermute | solution.py:479
  17.8 6.2 %collective-permute-start.1 = (f32[90,8,128]{2,1,0:T(8,128)S(1)}, f32[90,8,128]{2,1,0:T(8,128)S(1)}, u32[]{:S(2)}, u32[]{:S(2)}) collective-permute-start(f32[90,8,128]{2,1,0:T(8,128)S(1)} %get-tuple-element.24), channel_id=1, source_target_pairs={{0,0},{2,4},{4,2},{6,8},{8,6},{10,12},{12,10},{14,16},{16,14},{18,... | collective-permute-start | bytes 1105928 | tf_op jit(solution)/shard_map/ppermute | solution.py:422
  24.0 0.1 collective-permute-start
  24.1 0.0 collective-permute-done.8
  24.1 1.3 %collective-permute-start.9 = (f32[2,64,128]{2,1,0:T(8,128)S(1)}, f32[2,64,128]{2,1,0:T(8,128)S(1)}, u32[]{:S(2)}, u32[]{:S(2)}) collective-permute-start(f32[2,64,128]{2,1,0:T(8,128)S(1)} %add.10), channel_id=1, source_target_pairs={{0,4},{2,6},{4,0},{6,2},{8,12},{10,14},{12,8},{14,10},{16,20},{18,... | collective-permute-start | bytes 196616 | tf_op jit(solution)/shard_map/ppermute | solution.py:417
  25.4 4.4 %collective-permute-done.9 = f32[2,64,128]{2,1,0:T(8,128)S(1)} collective-permute-done((f32[2,64,128]{2,1,0:T(8,128)S(1)}, f32[2,64,128]{2,1,0:T(8,128)S(1)}, u32[]{:S(2)}, u32[]{:S(2)}) %collective-permute-start.9) | collective-permute-done | bytes 65568 | tf_op jit(solution)/shard_map/ppermute | solution.py:417
  29.8 3.3 %collective-permute-start.10 = (f32[2,64,128]{2,1,0:T(8,128)S(1)}, f32[2,64,128]{2,1,0:T(8,128)S(1)}, u32[]{:S(2)}, u32[]{:S(2)}) collective-permute-start(f32[2,64,128]{2,1,0:T(8,128)S(1)} %add.11.m0), channel_id=1, source_target_pairs={{0,12},{2,14},{4,8},{6,10},{8,4},{10,6},{12,0},{14,2},{16,28},{18,... | collective-permute-start | bytes 196616 | tf_op jit(solution)/shard_map/ppermute | solution.py:417
  33.1 1.7 %collective-permute-done.10.m1 = f32[2,64,128]{2,1,0:T(8,128)S(1)} collective-permute-done((f32[2,64,128]{2,1,0:T(8,128)S(1)}, f32[2,64,128]{2,1,0:T(8,128)S(1)}, u32[]{:S(2)}, u32[]{:S(2)}) %collective-permute-start.10) | collective-permute-done | bytes 65568 | tf_op jit(solution)/shard_map/ppermute | solution.py:417
  34.7 0.3 shard_map.101
  35.0 0.8 %collective-permute-start.11 = (f32[2,2,16,128]{3,2,1,0:T(8,128)S(1)}, f32[2,2,16,128]{3,2,1,0:T(8,128)S(1)}, u32[]{:S(2)}, u32[]{:S(2)}) collective-permute-start(f32[2,2,16,128]{3,2,1,0:T(8,128)S(1)} %get-tuple-element.36), channel_id=1, source_target_pairs={{0,16},{2,18},{4,20},{6,22},{8,24},{10,26},{12,28},{14,30},{16,0},... | collective-permute-start | bytes 98312 | tf_op jit(solution)/shard_map/ppermute | solution.py:417
  35.8 0.7 %collective-permute-start.3 = (f32[45,8,128]{2,1,0:T(8,128)S(1)}, f32[45,8,128]{2,1,0:T(8,128)S(1)}, u32[]{:S(2)}, u32[]{:S(2)}) collective-permute-start(f32[45,8,128]{2,1,0:T(8,128)S(1)} %get-tuple-element.25), channel_id=1, source_target_pairs={{0,56},{2,2},{4,60},{6,6},{8,8},{10,10},{12,12},{14,14},{16,16},{1... | collective-permute-start | bytes 552968 | tf_op jit(solution)/shard_map/ppermute | solution.py:422
  36.5 1.4 %collective-permute-done.11.second.far = f32[2,2,16,128]{3,2,1,0:T(8,128)S(1)} collective-permute-done((f32[2,2,16,128]{3,2,1,0:T(8,128)S(1)}, f32[2,2,16,128]{3,2,1,0:T(8,128)S(1)}, u32[]{:S(2)}, u32[]{:S(2)}) %collective-permute-start.11) | collective-permute-done | bytes 32800 | tf_op jit(solution)/shard_map/ppermute | solution.py:417
  37.9 0.7 %collective-permute-start.2 = (f32[45,8,128]{2,1,0:T(8,128)S(1)}, f32[45,8,128]{2,1,0:T(8,128)S(1)}, u32[]{:S(2)}, u32[]{:S(2)}) collective-permute-start(f32[45,8,128]{2,1,0:T(8,128)S(1)} %get-tuple-element.25), channel_id=1, source_target_pairs={{0,64},{2,2},{4,68},{6,6},{8,8},{10,10},{12,12},{14,14},{16,16},{1... | collective-permute-start | bytes 552968 | tf_op jit(solution)/shard_map/ppermute | solution.py:422
  38.5 0.0 collective-permute-done.3.wrap1
  38.6 10.0 %collective-permute-start.12 = (f32[2,2,16,128]{3,2,1,0:T(8,128)S(1)}, f32[2,2,16,128]{3,2,1,0:T(8,128)S(1)}, u32[]{:S(2)}, u32[]{:S(2)}) collective-permute-start(f32[2,2,16,128]{3,2,1,0:T(8,128)S(1)} %shard_map.102), channel_id=1, source_target_pairs={{0,2},{2,0},{4,6},{6,4},{8,10},{10,8},{12,14},{14,12},{16,18},{18,... | collective-permute-start | bytes 98312 | tf_op jit(solution)/shard_map/ppermute | solution.py:417
  48.6 1.8 %shard_map.94 = (f32[45,128,128]{2,1,0:T(8,128)S(1)}, f32[45,128,128]{2,1,0:T(8,128)S(1)}) custom-call(f32[99,8,128]{2,1,0:T(8,128)S(1)} %get-tuple-element.23.coef, f32[45,240,128]{2,1,0:T(8,128)S(1)} %get-tuple-element.22.x.x_in, f32[45,128,128]{2,1,0:T(8,128)} %bitcast.6), custom_call_target="tpu_custom_call" | custom-call | flops 10000000 | bytes 1250000 | tf_op jit(solution)/shard_map/pallas_call | solution.py:492
  50.4 1.1 %shard_map.95.out_in = f32[45,128,128]{2,1,0:T(8,128)S(1)} custom-call(f32[99,8,128]{2,1,0:T(8,128)S(1)} %get-tuple-element.23.coef, f32[45,240,128]{2,1,0:T(8,128)S(1)} %get-tuple-element.22.x.x_in, f32[45,128,128]{2,1,0:T(8,128)S(1)} %get-tuple-element.29.refs_0_), custom_call_target="tpu_custom_call", output_to_operand_aliasing={{}: (2, {})} | custom-call | flops 9000000 | bytes 1125000 | tf_op jit(solution)/shard_map/pallas_call | solution.py:501
  51.5 0.0 collective-permute-done.2.wrap0
  51.5 0.0 collective-permute-done.4.edge
  51.5 0.0 collective-permute-done.1.chip
  51.5 0.0 collective-permute-done.core
  51.5 0.2 shard_map.93.x
  51.7 0.4 shard_map.96.out_in
  52.1 1.7 %shard_map.97.out_in = f32[45,128,128]{2,1,0:T(8,128)S(1)} custom-call(f32[99,8,128]{2,1,0:T(8,128)S(1)} %get-tuple-element.23.coef, f32[45,240,128]{2,1,0:T(8,128)S(1)} %shard_map.93.x, f32[128,128]{1,0:T(8,128)S(1)} %get-tuple-element.27.dt, f32[45,128,128]{2,1,0:T(8,128)S(1)} %get-tuple-element.28.base, ...), custom_call_target="tpu_custom_call", output_to_operand_aliasing={{}: (4, {})} | custom-call | flops 20000000 | bytes 2500000 | tf_op jit(solution)/shard_map/pallas_call | solution.py:513
  53.8 1.2 %shard_map.98.acc = f32[45,128,128]{2,1,0:T(8,128)S(1)} custom-call(f32[99,8,128]{2,1,0:T(8,128)S(1)} %get-tuple-element.23.coef, f32[45,240,128]{2,1,0:T(8,128)S(1)} %shard_map.93.x, f32[128,128]{1,0:T(8,128)S(1)} %get-tuple-element.27.dt, f32[45,128,128]{2,1,0:T(8,128)S(1)} %get-tuple-element.28.base, ...), custom_call_target="tpu_custom_call", output_to_operand_aliasing={{}: (4, {})} | custom-call | flops 15000000 | bytes 1875000 | tf_op jit(solution)/shard_map/pallas_call | solution.py:513
  55.0 0.0 collective-permute-done.12.core
  55.0 2.8 %shard_map.103 = f32[45,128,128]{2,1,0:T(8,128)} custom-call(f32[45,128,128]{2,1,0:T(8,128)S(1)} %shard_map.98.acc, f32[2,16,128]{2,1,0:T(8,128)S(1)} %get-tuple-element.34.own, f32[2,2,16,128]{3,2,1,0:T(8,128)S(1)} %collective-permute-done.12.core, f32[2,2,16,128]{3,2,1,0:T(8,128)S(1)} %collective-permute-done.11.second.far, ...), custom_call_target="tpu_custom_call" | custom-call | flops 10000000 | bytes 1250000 | tf_op jit(solution)/shard_map/pallas_call | solution.py:527
  (5 shorter events, 0.0 us)
Async XLA Ops:
  2.4 2.3 %collective-permute-start.5 = (f32[2,2,16,128]{3,2,1,0:T(8,128)S(1)}, f32[2,2,16,128]{3,2,1,0:T(8,128)S(1)}, u32[]{:S(2)}, u32[]{:S(2)}) collective-permute-start(f32[2,2,16,128]{3,2,1,0:T(8,128)S(1)} %get-tuple-element.31), channel_id=1, source_target_pairs={{0,2},{2,0},{4,6},{6,4},{8,10},{10,8},{12,14},{14,12},{16,18},{18,... | collective-permute-start | bytes 98312 | tf_op jit(solution)/shard_map/ppermute | solution.py:417
  4.7 3.0 %collective-permute-start.6 = (f32[2,2,16,128]{3,2,1,0:T(8,128)S(1)}, f32[2,2,16,128]{3,2,1,0:T(8,128)S(1)}, u32[]{:S(2)}, u32[]{:S(2)}) collective-permute-start(f32[2,2,16,128]{3,2,1,0:T(8,128)S(1)} %shard_map.99), channel_id=1, source_target_pairs={{0,16},{2,18},{4,20},{6,22},{8,24},{10,26},{12,28},{14,30},{16,0},... | collective-permute-start | bytes 98312 | tf_op jit(solution)/shard_map/ppermute | solution.py:417
  8.0 3.4 %collective-permute-start.7 = (f32[2,64,128]{2,1,0:T(8,128)S(1)}, f32[2,64,128]{2,1,0:T(8,128)S(1)}, u32[]{:S(2)}, u32[]{:S(2)}) collective-permute-start(f32[2,64,128]{2,1,0:T(8,128)S(1)} %shard_map.100), channel_id=1, source_target_pairs={{0,32},{2,34},{4,36},{6,38},{8,40},{10,42},{12,44},{14,46},{16,48}... | collective-permute-start | bytes 196616 | tf_op jit(solution)/shard_map/ppermute | solution.py:417
  11.3 12.7 %collective-permute-start.8 = (f32[2,64,128]{2,1,0:T(8,128)S(1)}, f32[2,64,128]{2,1,0:T(8,128)S(1)}, u32[]{:S(2)}, u32[]{:S(2)}) collective-permute-start(f32[2,64,128]{2,1,0:T(8,128)S(1)} %add.9), channel_id=1, source_target_pairs={{0,96},{2,98},{4,100},{6,102},{8,104},{10,106},{12,108},{14,110},{... | collective-permute-start | bytes 196616 | tf_op jit(solution)/shard_map/ppermute | solution.py:417
  15.0 36.5 %collective-permute-start.4 = (f32[45,16,128]{2,1,0:T(8,128)S(1)}, f32[45,16,128]{2,1,0:T(8,128)S(1)}, u32[]{:S(2)}, u32[]{:S(2)}) collective-permute-start(f32[45,16,128]{2,1,0:T(8,128)S(1)} %get-tuple-element.26), channel_id=1, source_target_pairs={{0,1},{1,0},{2,3},{3,2},{4,5},{5,4},{6,7},{7,6},{8,9},{9,8},{10,11... | collective-permute-start | bytes 1105928 | tf_op jit(solution)/shard_map/ppermute | solution.py:479
  17.8 33.7 %collective-permute-start.1 = (f32[90,8,128]{2,1,0:T(8,128)S(1)}, f32[90,8,128]{2,1,0:T(8,128)S(1)}, u32[]{:S(2)}, u32[]{:S(2)}) collective-permute-start(f32[90,8,128]{2,1,0:T(8,128)S(1)} %get-tuple-element.24), channel_id=1, source_target_pairs={{0,0},{2,4},{4,2},{6,8},{8,6},{10,12},{12,10},{14,16},{16,14},{18,... | collective-permute-start | bytes 1105928 | tf_op jit(solution)/shard_map/ppermute | solution.py:422
  24.0 27.5 %collective-permute-start = (f32[90,8,128]{2,1,0:T(8,128)S(1)}, f32[90,8,128]{2,1,0:T(8,128)S(1)}, u32[]{:S(2)}, u32[]{:S(2)}) collective-permute-start(f32[90,8,128]{2,1,0:T(8,128)S(1)} %get-tuple-element.24), channel_id=1, source_target_pairs={{0,2},{2,0},{4,6},{6,4},{8,10},{10,8},{12,14},{14,12},{16,18},{18,... | collective-permute-start | bytes 1105928 | tf_op jit(solution)/shard_map/ppermute | solution.py:417
  24.1 5.7 %collective-permute-start.9 = (f32[2,64,128]{2,1,0:T(8,128)S(1)}, f32[2,64,128]{2,1,0:T(8,128)S(1)}, u32[]{:S(2)}, u32[]{:S(2)}) collective-permute-start(f32[2,64,128]{2,1,0:T(8,128)S(1)} %add.10), channel_id=1, source_target_pairs={{0,4},{2,6},{4,0},{6,2},{8,12},{10,14},{12,8},{14,10},{16,20},{18,... | collective-permute-start | bytes 196616 | tf_op jit(solution)/shard_map/ppermute | solution.py:417
  29.8 4.9 %collective-permute-start.10 = (f32[2,64,128]{2,1,0:T(8,128)S(1)}, f32[2,64,128]{2,1,0:T(8,128)S(1)}, u32[]{:S(2)}, u32[]{:S(2)}) collective-permute-start(f32[2,64,128]{2,1,0:T(8,128)S(1)} %add.11.m0), channel_id=1, source_target_pairs={{0,12},{2,14},{4,8},{6,10},{8,4},{10,6},{12,0},{14,2},{16,28},{18,... | collective-permute-start | bytes 196616 | tf_op jit(solution)/shard_map/ppermute | solution.py:417
  35.0 2.8 %collective-permute-start.11 = (f32[2,2,16,128]{3,2,1,0:T(8,128)S(1)}, f32[2,2,16,128]{3,2,1,0:T(8,128)S(1)}, u32[]{:S(2)}, u32[]{:S(2)}) collective-permute-start(f32[2,2,16,128]{3,2,1,0:T(8,128)S(1)} %get-tuple-element.36), channel_id=1, source_target_pairs={{0,16},{2,18},{4,20},{6,22},{8,24},{10,26},{12,28},{14,30},{16,0},... | collective-permute-start | bytes 98312 | tf_op jit(solution)/shard_map/ppermute | solution.py:417
  35.8 2.8 %collective-permute-start.3 = (f32[45,8,128]{2,1,0:T(8,128)S(1)}, f32[45,8,128]{2,1,0:T(8,128)S(1)}, u32[]{:S(2)}, u32[]{:S(2)}) collective-permute-start(f32[45,8,128]{2,1,0:T(8,128)S(1)} %get-tuple-element.25), channel_id=1, source_target_pairs={{0,56},{2,2},{4,60},{6,6},{8,8},{10,10},{12,12},{14,14},{16,16},{1... | collective-permute-start | bytes 552968 | tf_op jit(solution)/shard_map/ppermute | solution.py:422
  37.9 13.6 %collective-permute-start.2 = (f32[45,8,128]{2,1,0:T(8,128)S(1)}, f32[45,8,128]{2,1,0:T(8,128)S(1)}, u32[]{:S(2)}, u32[]{:S(2)}) collective-permute-start(f32[45,8,128]{2,1,0:T(8,128)S(1)} %get-tuple-element.25), channel_id=1, source_target_pairs={{0,64},{2,2},{4,68},{6,6},{8,8},{10,10},{12,12},{14,14},{16,16},{1... | collective-permute-start | bytes 552968 | tf_op jit(solution)/shard_map/ppermute | solution.py:422
  38.6 16.5 %collective-permute-start.12 = (f32[2,2,16,128]{3,2,1,0:T(8,128)S(1)}, f32[2,2,16,128]{3,2,1,0:T(8,128)S(1)}, u32[]{:S(2)}, u32[]{:S(2)}) collective-permute-start(f32[2,2,16,128]{3,2,1,0:T(8,128)S(1)} %shard_map.102), channel_id=1, source_target_pairs={{0,2},{2,0},{4,6},{6,4},{8,10},{10,8},{12,14},{14,12},{16,18},{18,... | collective-permute-start | bytes 98312 | tf_op jit(solution)/shard_map/ppermute | solution.py:417

commit v2 on v1

--- a/solution.py
+++ b/solution.py
@@ -23,7 +23,8 @@
 
 
 ALONG = ((0, 5), (5, 8))
-ACROSS = ((0, 1), (1, 5), (5, 8))
+ACROSS = ((0, 3), (3, 7))
+LAST = (7, 8)
 CENTRE, WAVE, SPAN, LEFT, RIGHT, COEFS = 90, 91, 95, 97, 98, 99
 
 
@@ -39,10 +40,6 @@
     return (
         (lax.axis_index("blk_0") * 2 + lax.axis_index("blk_1")) * 4 + lax.axis_index("blk_2")
     ) * 2 + lax.axis_index("blk_3")
-
-
-def own_quarter():
-    return lax.axis_index("blk_1") * 2 + lax.axis_index("blk_3")
 
 
 def lengths_of(order):
@@ -287,6 +284,11 @@
         far[1, i] = ghost[48:]
 
 
+def cells_of(place):
+    core = lax.axis_index("blk_3")
+    return 2 * jnp.where(place < 4, core, 1 - core) + (place & 1) + 4 * ((place >> 1) & 1)
+
+
 def ghosts_kernel(coef, core, chip, wrap0, wrap1, edge, x_in, x):
     left, right = coef[LEFT], coef[RIGHT]
     keep_low = jnp.concatenate([coef[SPAN]] * 2, axis=0)
@@ -310,7 +312,8 @@
 
 def across_kernel(first, last, coef, x, dt, base, out_in, out):
     @pl.loop(first, last)
-    def _(s):
+    def _(place):
+        s = cells_of(place)
         at = pl.multiple_of(24 * s + 32, 8)
         to = pl.multiple_of(16 * s, 16)
         for h in range(2):
@@ -388,29 +391,73 @@
                     out[u * 9 + k, there, :] = acc[u] + part
 
 
-def finish_kernel(acc, own, core, far, faces, mixing, dt, out_hbm, out, ghost, sem):
-    q = own_quarter()
-    for d, ref in enumerate((own, core.at[0], far.at[0], core.at[1])):
+def add_ghosts(places, refs, faces, mixing, dt, acc, stage, ghost, after):
+    cells = [cells_of(p) for p in places]
+    for n, (s, ref) in enumerate(zip(cells, refs)):
+        ghost[pl.ds(16 * n, 16), :] = ref[...] - faces[s]
+    terms = jnp.dot(ghost[...], mixing[...], precision=EXACT, preferred_element_type=F32)
+    lane = lax.broadcasted_iota(jnp.int32, (16, 128), 1)
+    rows = [pl.ds(pl.multiple_of(16 * s, 16), 16) for s in cells]
+    steps = [jnp.where((lane == 0) | (lane == 127), dt[r, :], 0.0) for r in rows]
+    for v in range(5):
+        for j in range(9 * v, 9 * v + 9):
+            turned = pltpu.roll(terms, 127 - 2 * j, 1)
+            for n in range(4):
+                stage[j, pl.ds(16 * n, 16), :] = (
+                    acc[j, rows[n], :] - steps[n] * turned[16 * n : 16 * n + 16]
+                )
+
+        after(v)
+
+
+def writes(stage, out_hbm, sem, first, variables):
+    core = lax.axis_index("blk_3")
+    core = core if first else 1 - core
+    lines = pl.ds(9 * variables[0], 9 * len(variables))
+    return [
+        pltpu.make_async_copy(
+            stage.at[lines, pl.ds(32 * n, 32), :],
+            out_hbm.at[lines, pl.ds(pl.multiple_of(32 * core + 64 * n, 32), 32), :],
+            sem.at[variables[0], n],
+        )
+        for n in range(2)
+    ]
+
+
+def near_kernel(
+    first, last, coef, x, dt, base, acc_in, own, far, faces, mixing,
+    acc, out_hbm, stage, ghost, sem,
+):
+    def send(v):
+        for copy in writes(stage, out_hbm, sem, True, (v,)):
+            copy.start()
+
+    refs = []
+    for half in range(2):
+        mine = (lax.axis_index("blk_1") == half)
         for i in range(2):
-            s = 2 * lax.bitwise_xor(q, d) + i
-            ghost[pl.ds(pl.multiple_of(16 * s, 16), 16), :] = ref[i] - faces[s]
-    terms = jnp.dot(ghost[...], mixing[...], precision=EXACT, preferred_element_type=F32)
-    lane = lax.broadcasted_iota(jnp.int32, (128, 128), 1)
-    step = jnp.where((lane == 0) | (lane == 127), dt[...], 0.0)
+            refs.append(jnp.where(mine, own[i], far[0, i]))
+    add_ghosts(range(4), refs, faces, mixing, dt, acc, stage, ghost, send)
+    across_kernel(first, last, coef, x, dt, base, None, acc)
     for v in range(5):
-        @pl.loop(9 * v, 9 * v + 9, step=3)
-        def _(first):
-            for j in (first, first + 1, first + 2):
-                turned = pltpu.roll(terms, 127 - 2 * j, 1)
-                out[j] = acc[j] - step * turned
-
-        pltpu.make_async_copy(
-            out.at[pl.ds(9 * v, 9)], out_hbm.at[pl.ds(9 * v, 9)], sem.at[v]
-        ).start()
+        for copy in writes(stage, out_hbm, sem, True, (v,)):
+            copy.wait()
+
+
+def finish_kernel(acc, core, faces, mixing, dt, out_in, out_hbm, stage, ghost, sem):
+    def send(v):
+        for copy in writes(stage, out_hbm, sem, False, (v,)):
+            copy.start()
+
+    refs = []
+    for half in range(2):
+        mine = (lax.axis_index("blk_1") == half)
+        for i in range(2):
+            refs.append(jnp.where(mine, core[0, i], core[1, i]))
+    add_ghosts(range(4, 8), refs, faces, mixing, dt, acc, stage, ghost, send)
     for v in range(5):
-        pltpu.make_async_copy(
-            out.at[pl.ds(9 * v, 9)], out_hbm.at[pl.ds(9 * v, 9)], sem.at[v]
-        ).wait()
+        for copy in writes(stage, out_hbm, sem, False, (v,)):
+            copy.wait()
 
 
 def swap(x, mask):
@@ -524,14 +571,25 @@
     far = swap(far, 8)
     core = call(pack_kernel, pair, [vspec()] * 2, vspec())(core, far)
     core = swap(core, 1)
+    half = [VMEM((45, 64, 128), F32), VMEM((64, 128), F32), dma((5, 2))]
+    acc, out = call(
+        functools.partial(near_kernel, *LAST),
+        [whole, sds(45, 128, 128)],
+        [vspec()] * 9,
+        [vspec(), hspec()],
+        half,
+        flops=15000000,
+        aliases={4: 0},
+    )(coef, x, dt, b, acc, own, far, faces, mixing)
     out = call(
         finish_kernel,
         sds(45, 128, 128),
-        [vspec()] * 7,
+        [vspec()] * 5 + [hspec()],
         hspec(),
-        [VMEM((45, 128, 128), F32), VMEM((128, 128), F32), dma((5,))],
-        flops=10000000,
-    )(acc, own, core, far, faces, mixing, dt)
+        half,
+        flops=5000000,
+        aliases={5: 0},
+    )(acc, core, faces, mixing, dt, out)
     return out.reshape(shape)
 
 

time: 58.2 us -> 58.4 us (level)
    pallas_call x1 -> x2, Pallas kernels: 2.85 us -> 3.35 us  [the longest x1 1.75 us: per_device(): call(functools.partial(near_kernel, *LAST), [whole, sds(45, 128, 128)], [...]
    pallas_call x3 -> x2, Pallas kernels: 3.32 us -> 3.05 us  [per_device(): call(functools.partial(across_kernel, first, last), whole, [vspec()] * 5,...]
  transfers between devices with their start and end apart: 13 -> 13, of which waited for: 5 -> 5; matrix products, arithmetic and copies ran while one was open for 0% -> 0% of each run, Pallas kernels for 14% -> 17%
where the time goes in v2:
time: 58.4 us; the launch traced here: 58.1 us
  starting transfers between devices  34 us (58%)
  Pallas kernels  13.9 us (24%)
  waiting for transfers between devices  10 us (17%)
    ppermute x9, starting transfers between devices, swap(): return lax.ppermute(x, BLK, [(i, i ^ mask) for i in range(64)])  23.7 us
    ppermute x9, waiting for transfers between devices, swap(): return lax.ppermute(x, BLK, [(i, i ^ mask) for i in range(64)])  10 us
    ppermute x3, starting transfers between devices, other_end(): return lax.ppermute(x, BLK, [(i, ends.get(i, i)) for i in range(64)])  7.52 us
    pallas_call x2, Pallas kernels, per_device(): call(functools.partial(across_kernel, first, last), whole, [vspec()] * 5,...  3.05 us
    ppermute x1, starting transfers between devices, per_device(): from_span = lax.ppermute(edge, 'span', [(0, 1), (1, 0)])  2.77 us
    pallas_call x1, Pallas kernels, per_device(): call(faces_kernel, [pair, pair, sds(8, 16, 128), padded], [hspec()], [vsp...  2.37 us
    pallas_call x1, Pallas kernels, per_device(): call(functools.partial(along_first_kernel, *ALONG[0]), [whole, whole], [v...  1.84 us
    pallas_call x1, Pallas kernels, per_device(): call(functools.partial(near_kernel, *LAST), [whole, sds(45, 128, 128)], [...  1.75 us
  transfers between devices with their start and end apart: 13, of which 5 were waited for; matrix products, arithmetic and copies ran while one was open for 0% of the time, Pallas kernels for 17%

profile of v2, /device:TPU:1, one launch (start us, length us, event | category | flops | bytes accessed | tf_op | source)
XLA Modules:
  0.0 58.1 jit_solution(8290795282413135226)
XLA Ops:
  0.0 2.4 %shard_map.91 = (f32[2,2,16,128]{3,2,1,0:T(8,128)S(1)}, f32[2,2,16,128]{3,2,1,0:T(8,128)S(1)}, f32[8,16,128]{2,1,0:T(8,128)S(1)}, f32[45,240,128]{2,1,0:T(8,128)S(1)}) custom-call(f32[45,128,128]{2,1,0:T(8,128)} %bitcast.5), custom_call_target="tpu_custom_call" | custom-call | tf_op jit(solution)/shard_map/pallas_call | solution.py:503
  2.4 1.5 %collective-permute-start.5 = (f32[2,2,16,128]{3,2,1,0:T(8,128)S(1)}, f32[2,2,16,128]{3,2,1,0:T(8,128)S(1)}, u32[]{:S(2)}, u32[]{:S(2)}) collective-permute-start(f32[2,2,16,128]{3,2,1,0:T(8,128)S(1)} %get-tuple-element.33), channel_id=1, source_target_pairs={{0,2},{2,0},{4,6},{6,4},{8,10},{10,8},{12,14},{14,12},{16,18},{18,... | collective-permute-start | bytes 98312 | tf_op jit(solution)/shard_map/ppermute | solution.py:464
  3.8 0.9 %collective-permute-done.5.other = f32[2,2,16,128]{3,2,1,0:T(8,128)S(1)} collective-permute-done((f32[2,2,16,128]{3,2,1,0:T(8,128)S(1)}, f32[2,2,16,128]{3,2,1,0:T(8,128)S(1)}, u32[]{:S(2)}, u32[]{:S(2)}) %collective-permute-start.5) | collective-permute-done | bytes 32800 | tf_op jit(solution)/shard_map/ppermute | solution.py:464
  4.7 1.4 %collective-permute-start.6 = (f32[2,2,16,128]{3,2,1,0:T(8,128)S(1)}, f32[2,2,16,128]{3,2,1,0:T(8,128)S(1)}, u32[]{:S(2)}, u32[]{:S(2)}) collective-permute-start(f32[2,2,16,128]{3,2,1,0:T(8,128)S(1)} %shard_map.98), channel_id=1, source_target_pairs={{0,16},{2,18},{4,20},{6,22},{8,24},{10,26},{12,28},{14,30},{16,0},... | collective-permute-start | bytes 98312 | tf_op jit(solution)/shard_map/ppermute | solution.py:464
  6.1 1.6 %shard_map.92 = (f32[90,8,128]{2,1,0:T(8,128)S(1)}, f32[45,8,128]{2,1,0:T(8,128)S(1)}, f32[45,16,128]{2,1,0:T(8,128)S(1)}, f32[96,64]{1,0:T(8,128)S(1)}, f32[128...) custom-call(s32[64]{0:T(128)} %rows_hbm.1, s32[3]{0:T(128)} %lag_hbm.1, ...), custom_call_target="tpu_custom_call" | custom-call | flops 2000000 | bytes 250000 | tf_op jit(solution)/shard_map/pallas_call | solution.py:509
  7.7 0.0 collective-permute-done.6.far
  7.7 0.2 shard_map.99
  8.0 1.7 %collective-permute-start.7 = (f32[2,64,128]{2,1,0:T(8,128)S(1)}, f32[2,64,128]{2,1,0:T(8,128)S(1)}, u32[]{:S(2)}, u32[]{:S(2)}) collective-permute-start(f32[2,64,128]{2,1,0:T(8,128)S(1)} %shard_map.99), channel_id=1, source_target_pairs={{0,32},{2,34},{4,36},{6,38},{8,40},{10,42},{12,44},{14,46},{16,48}... | collective-permute-start | bytes 196616 | tf_op jit(solution)/shard_map/ppermute | solution.py:464
  9.7 1.7 %collective-permute-done.7 = f32[2,64,128]{2,1,0:T(8,128)S(1)} collective-permute-done((f32[2,64,128]{2,1,0:T(8,128)S(1)}, f32[2,64,128]{2,1,0:T(8,128)S(1)}, u32[]{:S(2)}, u32[]{:S(2)}) %collective-permute-start.7) | collective-permute-done | bytes 65568 | tf_op jit(solution)/shard_map/ppermute | solution.py:464
  11.3 3.7 %collective-permute-start.8 = (f32[2,64,128]{2,1,0:T(8,128)S(1)}, f32[2,64,128]{2,1,0:T(8,128)S(1)}, u32[]{:S(2)}, u32[]{:S(2)}) collective-permute-start(f32[2,64,128]{2,1,0:T(8,128)S(1)} %add.9), channel_id=1, source_target_pairs={{0,96},{2,98},{4,100},{6,102},{8,104},{10,106},{12,108},{14,110},{... | collective-permute-start | bytes 196616 | tf_op jit(solution)/shard_map/ppermute | solution.py:464
  15.0 2.8 %collective-permute-start.4 = (f32[45,16,128]{2,1,0:T(8,128)S(1)}, f32[45,16,128]{2,1,0:T(8,128)S(1)}, u32[]{:S(2)}, u32[]{:S(2)}) collective-permute-start(f32[45,16,128]{2,1,0:T(8,128)S(1)} %get-tuple-element.28), channel_id=1, source_target_pairs={{0,1},{1,0},{2,3},{3,2},{4,5},{5,4},{6,7},{7,6},{8,9},{9,8},{10,11... | collective-permute-start | bytes 1105928 | tf_op jit(solution)/shard_map/ppermute | solution.py:526
  17.8 6.2 %collective-permute-start.1 = (f32[90,8,128]{2,1,0:T(8,128)S(1)}, f32[90,8,128]{2,1,0:T(8,128)S(1)}, u32[]{:S(2)}, u32[]{:S(2)}) collective-permute-start(f32[90,8,128]{2,1,0:T(8,128)S(1)} %get-tuple-element.26), channel_id=1, source_target_pairs={{0,0},{2,4},{4,2},{6,8},{8,6},{10,12},{12,10},{14,16},{16,14},{18,... | collective-permute-start | bytes 1105928 | tf_op jit(solution)/shard_map/ppermute | solution.py:469
  24.0 0.1 collective-permute-start
  24.1 0.0 collective-permute-done.8
  24.1 1.3 %collective-permute-start.9 = (f32[2,64,128]{2,1,0:T(8,128)S(1)}, f32[2,64,128]{2,1,0:T(8,128)S(1)}, u32[]{:S(2)}, u32[]{:S(2)}) collective-permute-start(f32[2,64,128]{2,1,0:T(8,128)S(1)} %add.10), channel_id=1, source_target_pairs={{0,4},{2,6},{4,0},{6,2},{8,12},{10,14},{12,8},{14,10},{16,20},{18,... | collective-permute-start | bytes 196616 | tf_op jit(solution)/shard_map/ppermute | solution.py:464
  25.4 4.4 %collective-permute-done.9 = f32[2,64,128]{2,1,0:T(8,128)S(1)} collective-permute-done((f32[2,64,128]{2,1,0:T(8,128)S(1)}, f32[2,64,128]{2,1,0:T(8,128)S(1)}, u32[]{:S(2)}, u32[]{:S(2)}) %collective-permute-start.9) | collective-permute-done | bytes 65568 | tf_op jit(solution)/shard_map/ppermute | solution.py:464
  29.8 3.3 %collective-permute-start.10 = (f32[2,64,128]{2,1,0:T(8,128)S(1)}, f32[2,64,128]{2,1,0:T(8,128)S(1)}, u32[]{:S(2)}, u32[]{:S(2)}) collective-permute-start(f32[2,64,128]{2,1,0:T(8,128)S(1)} %add.11.m0), channel_id=1, source_target_pairs={{0,12},{2,14},{4,8},{6,10},{8,4},{10,6},{12,0},{14,2},{16,28},{18,... | collective-permute-start | bytes 196616 | tf_op jit(solution)/shard_map/ppermute | solution.py:464
  33.1 1.7 %collective-permute-done.10.m1 = f32[2,64,128]{2,1,0:T(8,128)S(1)} collective-permute-done((f32[2,64,128]{2,1,0:T(8,128)S(1)}, f32[2,64,128]{2,1,0:T(8,128)S(1)}, u32[]{:S(2)}, u32[]{:S(2)}) %collective-permute-start.10) | collective-permute-done | bytes 65568 | tf_op jit(solution)/shard_map/ppermute | solution.py:464
  34.7 0.2 shard_map.100
  35.0 0.8 %collective-permute-start.11 = (f32[2,2,16,128]{3,2,1,0:T(8,128)S(1)}, f32[2,2,16,128]{3,2,1,0:T(8,128)S(1)}, u32[]{:S(2)}, u32[]{:S(2)}) collective-permute-start(f32[2,2,16,128]{3,2,1,0:T(8,128)S(1)} %get-tuple-element.37), channel_id=1, source_target_pairs={{0,16},{2,18},{4,20},{6,22},{8,24},{10,26},{12,28},{14,30},{16,0},... | collective-permute-start | bytes 98312 | tf_op jit(solution)/shard_map/ppermute | solution.py:464
  35.8 0.7 %collective-permute-start.3 = (f32[45,8,128]{2,1,0:T(8,128)S(1)}, f32[45,8,128]{2,1,0:T(8,128)S(1)}, u32[]{:S(2)}, u32[]{:S(2)}) collective-permute-start(f32[45,8,128]{2,1,0:T(8,128)S(1)} %get-tuple-element.27), channel_id=1, source_target_pairs={{0,56},{2,2},{4,60},{6,6},{8,8},{10,10},{12,12},{14,14},{16,16},{1... | collective-permute-start | bytes 552968 | tf_op jit(solution)/shard_map/ppermute | solution.py:469
  36.4 1.4 %collective-permute-done.11.far.second = f32[2,2,16,128]{3,2,1,0:T(8,128)S(1)} collective-permute-done((f32[2,2,16,128]{3,2,1,0:T(8,128)S(1)}, f32[2,2,16,128]{3,2,1,0:T(8,128)S(1)}, u32[]{:S(2)}, u32[]{:S(2)}) %collective-permute-start.11) | collective-permute-done | bytes 32800 | tf_op jit(solution)/shard_map/ppermute | solution.py:464
  37.8 0.7 %collective-permute-start.2 = (f32[45,8,128]{2,1,0:T(8,128)S(1)}, f32[45,8,128]{2,1,0:T(8,128)S(1)}, u32[]{:S(2)}, u32[]{:S(2)}) collective-permute-start(f32[45,8,128]{2,1,0:T(8,128)S(1)} %get-tuple-element.27), channel_id=1, source_target_pairs={{0,64},{2,2},{4,68},{6,6},{8,8},{10,10},{12,12},{14,14},{16,16},{1... | collective-permute-start | bytes 552968 | tf_op jit(solution)/shard_map/ppermute | solution.py:469
  38.5 0.0 collective-permute-done.3.wrap1
  38.5 10.0 %collective-permute-start.12 = (f32[2,2,16,128]{3,2,1,0:T(8,128)S(1)}, f32[2,2,16,128]{3,2,1,0:T(8,128)S(1)}, u32[]{:S(2)}, u32[]{:S(2)}) collective-permute-start(f32[2,2,16,128]{3,2,1,0:T(8,128)S(1)} %shard_map.102), channel_id=1, source_target_pairs={{0,2},{2,0},{4,6},{6,4},{8,10},{10,8},{12,14},{14,12},{16,18},{18,... | collective-permute-start | bytes 98312 | tf_op jit(solution)/shard_map/ppermute | solution.py:464
  48.6 1.8 %shard_map.94 = (f32[45,128,128]{2,1,0:T(8,128)S(1)}, f32[45,128,128]{2,1,0:T(8,128)S(1)}) custom-call(f32[99,8,128]{2,1,0:T(8,128)S(1)} %get-tuple-element.25.coef, f32[45,240,128]{2,1,0:T(8,128)S(1)} %get-tuple-element.24.x.x_in, f32[45,128,128]{2,1,0:T(8,128)} %bitcast.6), custom_call_target="tpu_custom_call" | custom-call | flops 10000000 | bytes 1250000 | tf_op jit(solution)/shard_map/pallas_call | solution.py:539
  50.4 1.1 %shard_map.95.out_in = f32[45,128,128]{2,1,0:T(8,128)S(1)} custom-call(f32[99,8,128]{2,1,0:T(8,128)S(1)} %get-tuple-element.25.coef, f32[45,240,128]{2,1,0:T(8,128)S(1)} %get-tuple-element.24.x.x_in, f32[45,128,128]{2,1,0:T(8,128)S(1)} %get-tuple-element.31.refs_0_), custom_call_target="tpu_custom_call", output_to_operand_aliasing={{}: (2, {})} | custom-call | flops 9000000 | bytes 1125000 | tf_op jit(solution)/shard_map/pallas_call | solution.py:548
  51.5 0.0 collective-permute-done.2.wrap0
  51.5 0.0 collective-permute-done.4.edge
  51.5 0.0 collective-permute-done.1.chip
  51.5 0.0 collective-permute-done.core
  51.5 0.2 shard_map.93.x
  51.7 1.3 %shard_map.96.out_in = f32[45,128,128]{2,1,0:T(8,128)S(1)} custom-call(f32[99,8,128]{2,1,0:T(8,128)S(1)} %get-tuple-element.25.coef, f32[45,240,128]{2,1,0:T(8,128)S(1)} %shard_map.93.x, f32[128,128]{1,0:T(8,128)S(1)} %get-tuple-element.29.dt, f32[45,128,128]{2,1,0:T(8,128)S(1)} %get-tuple-element.30.base, ...), custom_call_target="tpu_custom_call", output_to_operand_aliasing={{}: (4, {})} | custom-call | flops 15000000 | bytes 1875000 | tf_op jit(solution)/shard_map/pallas_call | solution.py:560
  53.0 1.7 %shard_map.97.acc_in = f32[45,128,128]{2,1,0:T(8,128)S(1)} custom-call(f32[99,8,128]{2,1,0:T(8,128)S(1)} %get-tuple-element.25.coef, f32[45,240,128]{2,1,0:T(8,128)S(1)} %shard_map.93.x, f32[128,128]{1,0:T(8,128)S(1)} %get-tuple-element.29.dt, f32[45,128,128]{2,1,0:T(8,128)S(1)} %get-tuple-element.30.base, ...), custom_call_target="tpu_custom_call", output_to_operand_aliasing={{}: (4, {})} | custom-call | flops 20000000 | bytes 2500000 | tf_op jit(solution)/shard_map/pallas_call | solution.py:560
  54.7 1.8 %shard_map.101 = (f32[45,128,128]{2,1,0:T(8,128)S(1)}, f32[45,128,128]{2,1,0:T(8,128)}) custom-call(f32[99,8,128]{2,1,0:T(8,128)S(1)} %get-tuple-element.25.coef, f32[45,240,128]{2,1,0:T(8,128)S(1)} %shard_map.93.x, f32[128,128]{1,0:T(8,128)S(1)} %get-tuple-element.29.dt, ...), custom_call_target="tpu_custom_call", output_to_operand_aliasing={{0}: (4, {})} | custom-call | flops 15000000 | bytes 1875000 | tf_op jit(solution)/shard_map/pallas_call | solution.py:575
  56.5 0.0 collective-permute-done.12.core
  56.5 1.6 %shard_map.103 = f32[45,128,128]{2,1,0:T(8,128)} custom-call(f32[45,128,128]{2,1,0:T(8,128)S(1)} %get-tuple-element.40.acc, f32[2,2,16,128]{3,2,1,0:T(8,128)S(1)} %collective-permute-done.12.core, f32[8,16,128]{2,1,0:T(8,128)S(1)} %get-tuple-element.38.faces, f32[128,128]{1,0:T(8,128)S(1)} %get-tuple-element.39.mixing, ...), custom_call_target="tpu_custom_call", output_to_operand_aliasing={{}: (5, {})} | custom-call | flops 5000000 | bytes 625000 | tf_op jit(solution)/shard_map/pallas_call | solution.py:584
  (5 shorter events, 0.0 us)
Async XLA Ops:
  2.4 2.3 %collective-permute-start.5 = (f32[2,2,16,128]{3,2,1,0:T(8,128)S(1)}, f32[2,2,16,128]{3,2,1,0:T(8,128)S(1)}, u32[]{:S(2)}, u32[]{:S(2)}) collective-permute-start(f32[2,2,16,128]{3,2,1,0:T(8,128)S(1)} %get-tuple-element.33), channel_id=1, source_target_pairs={{0,2},{2,0},{4,6},{6,4},{8,10},{10,8},{12,14},{14,12},{16,18},{18,... | collective-permute-start | bytes 98312 | tf_op jit(solution)/shard_map/ppermute | solution.py:464
  4.7 3.0 %collective-permute-start.6 = (f32[2,2,16,128]{3,2,1,0:T(8,128)S(1)}, f32[2,2,16,128]{3,2,1,0:T(8,128)S(1)}, u32[]{:S(2)}, u32[]{:S(2)}) collective-permute-start(f32[2,2,16,128]{3,2,1,0:T(8,128)S(1)} %shard_map.98), channel_id=1, source_target_pairs={{0,16},{2,18},{4,20},{6,22},{8,24},{10,26},{12,28},{14,30},{16,0},... | collective-permute-start | bytes 98312 | tf_op jit(solution)/shard_map/ppermute | solution.py:464
  8.0 3.4 %collective-permute-start.7 = (f32[2,64,128]{2,1,0:T(8,128)S(1)}, f32[2,64,128]{2,1,0:T(8,128)S(1)}, u32[]{:S(2)}, u32[]{:S(2)}) collective-permute-start(f32[2,64,128]{2,1,0:T(8,128)S(1)} %shard_map.99), channel_id=1, source_target_pairs={{0,32},{2,34},{4,36},{6,38},{8,40},{10,42},{12,44},{14,46},{16,48}... | collective-permute-start | bytes 196616 | tf_op jit(solution)/shard_map/ppermute | solution.py:464
  11.3 12.7 %collective-permute-start.8 = (f32[2,64,128]{2,1,0:T(8,128)S(1)}, f32[2,64,128]{2,1,0:T(8,128)S(1)}, u32[]{:S(2)}, u32[]{:S(2)}) collective-permute-start(f32[2,64,128]{2,1,0:T(8,128)S(1)} %add.9), channel_id=1, source_target_pairs={{0,96},{2,98},{4,100},{6,102},{8,104},{10,106},{12,108},{14,110},{... | collective-permute-start | bytes 196616 | tf_op jit(solution)/shard_map/ppermute | solution.py:464
  15.0 36.5 %collective-permute-start.4 = (f32[45,16,128]{2,1,0:T(8,128)S(1)}, f32[45,16,128]{2,1,0:T(8,128)S(1)}, u32[]{:S(2)}, u32[]{:S(2)}) collective-permute-start(f32[45,16,128]{2,1,0:T(8,128)S(1)} %get-tuple-element.28), channel_id=1, source_target_pairs={{0,1},{1,0},{2,3},{3,2},{4,5},{5,4},{6,7},{7,6},{8,9},{9,8},{10,11... | collective-permute-start | bytes 1105928 | tf_op jit(solution)/shard_map/ppermute | solution.py:526
  17.8 33.7 %collective-permute-start.1 = (f32[90,8,128]{2,1,0:T(8,128)S(1)}, f32[90,8,128]{2,1,0:T(8,128)S(1)}, u32[]{:S(2)}, u32[]{:S(2)}) collective-permute-start(f32[90,8,128]{2,1,0:T(8,128)S(1)} %get-tuple-element.26), channel_id=1, source_target_pairs={{0,0},{2,4},{4,2},{6,8},{8,6},{10,12},{12,10},{14,16},{16,14},{18,... | collective-permute-start | bytes 1105928 | tf_op jit(solution)/shard_map/ppermute | solution.py:469
  24.0 27.5 %collective-permute-start = (f32[90,8,128]{2,1,0:T(8,128)S(1)}, f32[90,8,128]{2,1,0:T(8,128)S(1)}, u32[]{:S(2)}, u32[]{:S(2)}) collective-permute-start(f32[90,8,128]{2,1,0:T(8,128)S(1)} %get-tuple-element.26), channel_id=1, source_target_pairs={{0,2},{2,0},{4,6},{6,4},{8,10},{10,8},{12,14},{14,12},{16,18},{18,... | collective-permute-start | bytes 1105928 | tf_op jit(solution)/shard_map/ppermute | solution.py:464
  24.1 5.7 %collective-permute-start.9 = (f32[2,64,128]{2,1,0:T(8,128)S(1)}, f32[2,64,128]{2,1,0:T(8,128)S(1)}, u32[]{:S(2)}, u32[]{:S(2)}) collective-permute-start(f32[2,64,128]{2,1,0:T(8,128)S(1)} %add.10), channel_id=1, source_target_pairs={{0,4},{2,6},{4,0},{6,2},{8,12},{10,14},{12,8},{14,10},{16,20},{18,... | collective-permute-start | bytes 196616 | tf_op jit(solution)/shard_map/ppermute | solution.py:464
  29.8 4.9 %collective-permute-start.10 = (f32[2,64,128]{2,1,0:T(8,128)S(1)}, f32[2,64,128]{2,1,0:T(8,128)S(1)}, u32[]{:S(2)}, u32[]{:S(2)}) collective-permute-start(f32[2,64,128]{2,1,0:T(8,128)S(1)} %add.11.m0), channel_id=1, source_target_pairs={{0,12},{2,14},{4,8},{6,10},{8,4},{10,6},{12,0},{14,2},{16,28},{18,... | collective-permute-start | bytes 196616 | tf_op jit(solution)/shard_map/ppermute | solution.py:464
  35.0 2.8 %collective-permute-start.11 = (f32[2,2,16,128]{3,2,1,0:T(8,128)S(1)}, f32[2,2,16,128]{3,2,1,0:T(8,128)S(1)}, u32[]{:S(2)}, u32[]{:S(2)}) collective-permute-start(f32[2,2,16,128]{3,2,1,0:T(8,128)S(1)} %get-tuple-element.37), channel_id=1, source_target_pairs={{0,16},{2,18},{4,20},{6,22},{8,24},{10,26},{12,28},{14,30},{16,0},... | collective-permute-start | bytes 98312 | tf_op jit(solution)/shard_map/ppermute | solution.py:464
  35.8 2.8 %collective-permute-start.3 = (f32[45,8,128]{2,1,0:T(8,128)S(1)}, f32[45,8,128]{2,1,0:T(8,128)S(1)}, u32[]{:S(2)}, u32[]{:S(2)}) collective-permute-start(f32[45,8,128]{2,1,0:T(8,128)S(1)} %get-tuple-element.27), channel_id=1, source_target_pairs={{0,56},{2,2},{4,60},{6,6},{8,8},{10,10},{12,12},{14,14},{16,16},{1... | collective-permute-start | bytes 552968 | tf_op jit(solution)/shard_map/ppermute | solution.py:469
  37.8 13.6 %collective-permute-start.2 = (f32[45,8,128]{2,1,0:T(8,128)S(1)}, f32[45,8,128]{2,1,0:T(8,128)S(1)}, u32[]{:S(2)}, u32[]{:S(2)}) collective-permute-start(f32[45,8,128]{2,1,0:T(8,128)S(1)} %get-tuple-element.27), channel_id=1, source_target_pairs={{0,64},{2,2},{4,68},{6,6},{8,8},{10,10},{12,12},{14,14},{16,16},{1... | collective-permute-start | bytes 552968 | tf_op jit(solution)/shard_map/ppermute | solution.py:469
  38.5 18.0 %collective-permute-start.12 = (f32[2,2,16,128]{3,2,1,0:T(8,128)S(1)}, f32[2,2,16,128]{3,2,1,0:T(8,128)S(1)}, u32[]{:S(2)}, u32[]{:S(2)}) collective-permute-start(f32[2,2,16,128]{3,2,1,0:T(8,128)S(1)} %shard_map.102), channel_id=1, source_target_pairs={{0,2},{2,0},{4,6},{6,4},{8,10},{10,8},{12,14},{14,12},{16,18},{18,... | collective-permute-start | bytes 98312 | tf_op jit(solution)/shard_map/ppermute | solution.py:464

commit v3 on v2

--- a/solution.py
+++ b/solution.py
@@ -18,13 +18,13 @@
 VMEM = pltpu.VMEM
 F32 = jnp.float32
 QUAD = (0, 1, 8, 9)
-HOPS = (16, 48, 2, 6)
+HOPS = (16, 48, 6, 2)
 DN = tuple(0.5 * math.cos(math.pi * n) / math.sin(math.pi * n / 9) for n in range(5) if n)
 
 
 ALONG = ((0, 5), (5, 8))
-ACROSS = ((0, 3), (3, 7))
-LAST = (7, 8)
+ACROSS = ((0, 4), (4, 8))
+LAST = (8, 8)
 CENTRE, WAVE, SPAN, LEFT, RIGHT, COEFS = 90, 91, 95, 97, 98, 99
 
 

time: 58.4 us -> 57 us (0.976)
  starting transfers between devices: 34 us -> 28.9 us
  waiting for transfers between devices: 10 us -> 13.5 us
    ppermute x9, starting transfers between devices: 23.7 us -> 18.6 us  [swap(): return lax.ppermute(x, BLK, [(i, i ^ mask) for i in range(64)])]
    ppermute x9, waiting for transfers between devices: 10 us -> 13.5 us  [swap(): return lax.ppermute(x, BLK, [(i, i ^ mask) for i in range(64)])]
  transfers between devices with their start and end apart: 13 -> 13, of which waited for: 5 -> 5; matrix products, arithmetic and copies ran while one was open for 0% -> 0% of each run, Pallas kernels for 17% -> 18%
where the time goes in v3:
time: 57 us; the launch traced here: 56.7 us
  starting transfers between devices  28.9 us (51%)
  Pallas kernels  14.1 us (25%)
  waiting for transfers between devices  13.5 us (24%)
    ppermute x9, starting transfers between devices, swap(): return lax.ppermute(x, BLK, [(i, i ^ mask) for i in range(64)])  18.6 us
    ppermute x9, waiting for transfers between devices, swap(): return lax.ppermute(x, BLK, [(i, i ^ mask) for i in range(64)])  13.5 us
    ppermute x3, starting transfers between devices, other_end(): return lax.ppermute(x, BLK, [(i, ends.get(i, i)) for i in range(64)])  7.52 us
    pallas_call x2, Pallas kernels, per_device(): call(functools.partial(across_kernel, first, last), whole, [vspec()] * 5,...  3.47 us
    ppermute x1, starting transfers between devices, per_device(): from_span = lax.ppermute(edge, 'span', [(0, 1), (1, 0)])  2.77 us
    pallas_call x1, Pallas kernels, per_device(): call(faces_kernel, [pair, pair, sds(8, 16, 128), padded], [hspec()], [vsp...  2.37 us
    pallas_call x1, Pallas kernels, per_device(): call(functools.partial(along_first_kernel, *ALONG[0]), [whole, whole], [v...  1.84 us
    pallas_call x1, Pallas kernels, per_device(): call(finish_kernel, sds(45, 128, 128), [vspec()] * 5 + [hspec()], hspec()...  1.59 us
  transfers between devices with their start and end apart: 13, of which 5 were waited for; matrix products, arithmetic and copies ran while one was open for 0% of the time, Pallas kernels for 18%

profile of v3, /device:TPU:1, one launch (start us, length us, event | category | flops | bytes accessed | tf_op | source)
XLA Modules:
  0.0 56.7 jit_solution(1285908606278398261)
XLA Ops:
  0.0 2.4 %shard_map.91 = (f32[2,2,16,128]{3,2,1,0:T(8,128)S(1)}, f32[2,2,16,128]{3,2,1,0:T(8,128)S(1)}, f32[8,16,128]{2,1,0:T(8,128)S(1)}, f32[45,240,128]{2,1,0:T(8,128)S(1)}) custom-call(f32[45,128,128]{2,1,0:T(8,128)} %bitcast.5), custom_call_target="tpu_custom_call" | custom-call | tf_op jit(solution)/shard_map/pallas_call | solution.py:503
  2.4 1.5 %collective-permute-start.5 = (f32[2,2,16,128]{3,2,1,0:T(8,128)S(1)}, f32[2,2,16,128]{3,2,1,0:T(8,128)S(1)}, u32[]{:S(2)}, u32[]{:S(2)}) collective-permute-start(f32[2,2,16,128]{3,2,1,0:T(8,128)S(1)} %get-tuple-element.33), channel_id=1, source_target_pairs={{0,2},{2,0},{4,6},{6,4},{8,10},{10,8},{12,14},{14,12},{16,18},{18,... | collective-permute-start | bytes 98312 | tf_op jit(solution)/shard_map/ppermute | solution.py:464
  3.8 0.9 %collective-permute-done.5.other = f32[2,2,16,128]{3,2,1,0:T(8,128)S(1)} collective-permute-done((f32[2,2,16,128]{3,2,1,0:T(8,128)S(1)}, f32[2,2,16,128]{3,2,1,0:T(8,128)S(1)}, u32[]{:S(2)}, u32[]{:S(2)}) %collective-permute-start.5) | collective-permute-done | bytes 32800 | tf_op jit(solution)/shard_map/ppermute | solution.py:464
  4.7 1.4 %collective-permute-start.6 = (f32[2,2,16,128]{3,2,1,0:T(8,128)S(1)}, f32[2,2,16,128]{3,2,1,0:T(8,128)S(1)}, u32[]{:S(2)}, u32[]{:S(2)}) collective-permute-start(f32[2,2,16,128]{3,2,1,0:T(8,128)S(1)} %shard_map.98), channel_id=1, source_target_pairs={{0,16},{2,18},{4,20},{6,22},{8,24},{10,26},{12,28},{14,30},{16,0},... | collective-permute-start | bytes 98312 | tf_op jit(solution)/shard_map/ppermute | solution.py:464
  6.1 1.6 %shard_map.92 = (f32[90,8,128]{2,1,0:T(8,128)S(1)}, f32[45,8,128]{2,1,0:T(8,128)S(1)}, f32[45,16,128]{2,1,0:T(8,128)S(1)}, f32[96,64]{1,0:T(8,128)S(1)}, f32[128...) custom-call(s32[64]{0:T(128)} %rows_hbm.1, s32[3]{0:T(128)} %lag_hbm.1, ...), custom_call_target="tpu_custom_call" | custom-call | flops 2000000 | bytes 250000 | tf_op jit(solution)/shard_map/pallas_call | solution.py:509
  7.7 0.0 collective-permute-done.6.far
  7.7 0.2 shard_map.99
  8.0 1.7 %collective-permute-start.7 = (f32[2,64,128]{2,1,0:T(8,128)S(1)}, f32[2,64,128]{2,1,0:T(8,128)S(1)}, u32[]{:S(2)}, u32[]{:S(2)}) collective-permute-start(f32[2,64,128]{2,1,0:T(8,128)S(1)} %shard_map.99), channel_id=1, source_target_pairs={{0,32},{2,34},{4,36},{6,38},{8,40},{10,42},{12,44},{14,46},{16,48}... | collective-permute-start | bytes 196616 | tf_op jit(solution)/shard_map/ppermute | solution.py:464
  9.7 1.7 %collective-permute-done.7 = f32[2,64,128]{2,1,0:T(8,128)S(1)} collective-permute-done((f32[2,64,128]{2,1,0:T(8,128)S(1)}, f32[2,64,128]{2,1,0:T(8,128)S(1)}, u32[]{:S(2)}, u32[]{:S(2)}) %collective-permute-start.7) | collective-permute-done | bytes 65568 | tf_op jit(solution)/shard_map/ppermute | solution.py:464
  11.3 3.7 %collective-permute-start.8 = (f32[2,64,128]{2,1,0:T(8,128)S(1)}, f32[2,64,128]{2,1,0:T(8,128)S(1)}, u32[]{:S(2)}, u32[]{:S(2)}) collective-permute-start(f32[2,64,128]{2,1,0:T(8,128)S(1)} %add.9), channel_id=1, source_target_pairs={{0,96},{2,98},{4,100},{6,102},{8,104},{10,106},{12,108},{14,110},{... | collective-permute-start | bytes 196616 | tf_op jit(solution)/shard_map/ppermute | solution.py:464
  15.0 2.8 %collective-permute-start.4 = (f32[45,16,128]{2,1,0:T(8,128)S(1)}, f32[45,16,128]{2,1,0:T(8,128)S(1)}, u32[]{:S(2)}, u32[]{:S(2)}) collective-permute-start(f32[45,16,128]{2,1,0:T(8,128)S(1)} %get-tuple-element.28), channel_id=1, source_target_pairs={{0,1},{1,0},{2,3},{3,2},{4,5},{5,4},{6,7},{7,6},{8,9},{9,8},{10,11... | collective-permute-start | bytes 1105928 | tf_op jit(solution)/shard_map/ppermute | solution.py:526
  17.8 6.2 %collective-permute-start.1 = (f32[90,8,128]{2,1,0:T(8,128)S(1)}, f32[90,8,128]{2,1,0:T(8,128)S(1)}, u32[]{:S(2)}, u32[]{:S(2)}) collective-permute-start(f32[90,8,128]{2,1,0:T(8,128)S(1)} %get-tuple-element.26), channel_id=1, source_target_pairs={{0,0},{2,4},{4,2},{6,8},{8,6},{10,12},{12,10},{14,16},{16,14},{18,... | collective-permute-start | bytes 1105928 | tf_op jit(solution)/shard_map/ppermute | solution.py:469
  24.0 0.1 collective-permute-start
  24.1 0.0 collective-permute-done.8
  24.1 1.7 %collective-permute-start.9 = (f32[2,64,128]{2,1,0:T(8,128)S(1)}, f32[2,64,128]{2,1,0:T(8,128)S(1)}, u32[]{:S(2)}, u32[]{:S(2)}) collective-permute-start(f32[2,64,128]{2,1,0:T(8,128)S(1)} %add.10), channel_id=1, source_target_pairs={{0,12},{2,14},{4,8},{6,10},{8,4},{10,6},{12,0},{14,2},{16,28},{18,... | collective-permute-start | bytes 196616 | tf_op jit(solution)/shard_map/ppermute | solution.py:464
  25.8 6.1 %collective-permute-done.9 = f32[2,64,128]{2,1,0:T(8,128)S(1)} collective-permute-done((f32[2,64,128]{2,1,0:T(8,128)S(1)}, f32[2,64,128]{2,1,0:T(8,128)S(1)}, u32[]{:S(2)}, u32[]{:S(2)}) %collective-permute-start.9) | collective-permute-done | bytes 65568 | tf_op jit(solution)/shard_map/ppermute | solution.py:464
  31.9 0.1 collective-permute-start.10
  32.0 3.2 %collective-permute-done.10.m1 = f32[2,64,128]{2,1,0:T(8,128)S(1)} collective-permute-done((f32[2,64,128]{2,1,0:T(8,128)S(1)}, f32[2,64,128]{2,1,0:T(8,128)S(1)}, u32[]{:S(2)}, u32[]{:S(2)}) %collective-permute-start.10) | collective-permute-done | bytes 65568 | tf_op jit(solution)/shard_map/ppermute | solution.py:464
  35.2 0.2 shard_map.100
  35.5 0.6 collective-permute-start.11
  36.0 0.7 %collective-permute-start.3 = (f32[45,8,128]{2,1,0:T(8,128)S(1)}, f32[45,8,128]{2,1,0:T(8,128)S(1)}, u32[]{:S(2)}, u32[]{:S(2)}) collective-permute-start(f32[45,8,128]{2,1,0:T(8,128)S(1)} %get-tuple-element.27), channel_id=1, source_target_pairs={{0,56},{2,2},{4,60},{6,6},{8,8},{10,10},{12,12},{14,14},{16,16},{1... | collective-permute-start | bytes 552968 | tf_op jit(solution)/shard_map/ppermute | solution.py:469
  36.7 1.6 %collective-permute-done.11.far.second = f32[2,2,16,128]{3,2,1,0:T(8,128)S(1)} collective-permute-done((f32[2,2,16,128]{3,2,1,0:T(8,128)S(1)}, f32[2,2,16,128]{3,2,1,0:T(8,128)S(1)}, u32[]{:S(2)}, u32[]{:S(2)}) %collective-permute-start.11) | collective-permute-done | bytes 32800 | tf_op jit(solution)/shard_map/ppermute | solution.py:464
  38.3 0.7 %collective-permute-start.2 = (f32[45,8,128]{2,1,0:T(8,128)S(1)}, f32[45,8,128]{2,1,0:T(8,128)S(1)}, u32[]{:S(2)}, u32[]{:S(2)}) collective-permute-start(f32[45,8,128]{2,1,0:T(8,128)S(1)} %get-tuple-element.27), channel_id=1, source_target_pairs={{0,64},{2,2},{4,68},{6,6},{8,8},{10,10},{12,12},{14,14},{16,16},{1... | collective-permute-start | bytes 552968 | tf_op jit(solution)/shard_map/ppermute | solution.py:469
  39.0 0.0 collective-permute-done.3.wrap1
  39.0 7.9 %collective-permute-start.12 = (f32[2,2,16,128]{3,2,1,0:T(8,128)S(1)}, f32[2,2,16,128]{3,2,1,0:T(8,128)S(1)}, u32[]{:S(2)}, u32[]{:S(2)}) collective-permute-start(f32[2,2,16,128]{3,2,1,0:T(8,128)S(1)} %shard_map.102), channel_id=1, source_target_pairs={{0,2},{2,0},{4,6},{6,4},{8,10},{10,8},{12,14},{14,12},{16,18},{18,... | collective-permute-start | bytes 98312 | tf_op jit(solution)/shard_map/ppermute | solution.py:464
  46.9 1.8 %shard_map.94 = (f32[45,128,128]{2,1,0:T(8,128)S(1)}, f32[45,128,128]{2,1,0:T(8,128)S(1)}) custom-call(f32[99,8,128]{2,1,0:T(8,128)S(1)} %get-tuple-element.25.coef, f32[45,240,128]{2,1,0:T(8,128)S(1)} %get-tuple-element.24.x.x_in, f32[45,128,128]{2,1,0:T(8,128)} %bitcast.6), custom_call_target="tpu_custom_call" | custom-call | flops 10000000 | bytes 1250000 | tf_op jit(solution)/shard_map/pallas_call | solution.py:539
  48.8 1.1 %shard_map.95.out_in = f32[45,128,128]{2,1,0:T(8,128)S(1)} custom-call(f32[99,8,128]{2,1,0:T(8,128)S(1)} %get-tuple-element.25.coef, f32[45,240,128]{2,1,0:T(8,128)S(1)} %get-tuple-element.24.x.x_in, f32[45,128,128]{2,1,0:T(8,128)S(1)} %get-tuple-element.31.refs_0_), custom_call_target="tpu_custom_call", output_to_operand_aliasing={{}: (2, {})} | custom-call | flops 9000000 | bytes 1125000 | tf_op jit(solution)/shard_map/pallas_call | solution.py:548
  49.8 0.0 collective-permute-done.2.wrap0
  49.8 0.0 collective-permute-done.4.edge
  49.9 0.0 collective-permute-done.1.chip
  49.9 0.0 collective-permute-done.core
  49.9 0.2 shard_map.93.x
  50.0 1.8 %shard_map.96.out_in = f32[45,128,128]{2,1,0:T(8,128)S(1)} custom-call(f32[99,8,128]{2,1,0:T(8,128)S(1)} %get-tuple-element.25.coef, f32[45,240,128]{2,1,0:T(8,128)S(1)} %shard_map.93.x, f32[128,128]{1,0:T(8,128)S(1)} %get-tuple-element.29.dt, f32[45,128,128]{2,1,0:T(8,128)S(1)} %get-tuple-element.30.base, ...), custom_call_target="tpu_custom_call", output_to_operand_aliasing={{}: (4, {})} | custom-call | flops 20000000 | bytes 2500000 | tf_op jit(solution)/shard_map/pallas_call | solution.py:560
  51.8 1.7 %shard_map.97.acc_in = f32[45,128,128]{2,1,0:T(8,128)S(1)} custom-call(f32[99,8,128]{2,1,0:T(8,128)S(1)} %get-tuple-element.25.coef, f32[45,240,128]{2,1,0:T(8,128)S(1)} %shard_map.93.x, f32[128,128]{1,0:T(8,128)S(1)} %get-tuple-element.29.dt, f32[45,128,128]{2,1,0:T(8,128)S(1)} %get-tuple-element.30.base, ...), custom_call_target="tpu_custom_call", output_to_operand_aliasing={{}: (4, {})} | custom-call | flops 20000000 | bytes 2500000 | tf_op jit(solution)/shard_map/pallas_call | solution.py:560
  53.5 1.6 %shard_map.101 = (f32[45,128,128]{2,1,0:T(8,128)S(1)}, f32[45,128,128]{2,1,0:T(8,128)}) custom-call(f32[99,8,128]{2,1,0:T(8,128)S(1)} %get-tuple-element.25.coef, f32[45,240,128]{2,1,0:T(8,128)S(1)} %shard_map.93.x, f32[128,128]{1,0:T(8,128)S(1)} %get-tuple-element.29.dt, ...), custom_call_target="tpu_custom_call", output_to_operand_aliasing={{0}: (4, {})} | custom-call | flops 15000000 | bytes 1875000 | tf_op jit(solution)/shard_map/pallas_call | solution.py:575
  55.1 0.0 collective-permute-done.12.core
  55.1 1.6 %shard_map.103 = f32[45,128,128]{2,1,0:T(8,128)} custom-call(f32[45,128,128]{2,1,0:T(8,128)S(1)} %get-tuple-element.40.acc, f32[2,2,16,128]{3,2,1,0:T(8,128)S(1)} %collective-permute-done.12.core, f32[8,16,128]{2,1,0:T(8,128)S(1)} %get-tuple-element.38.faces, f32[128,128]{1,0:T(8,128)S(1)} %get-tuple-element.39.mixing, ...), custom_call_target="tpu_custom_call", output_to_operand_aliasing={{}: (5, {})} | custom-call | flops 5000000 | bytes 625000 | tf_op jit(solution)/shard_map/pallas_call | solution.py:584
  (5 shorter events, 0.0 us)
Async XLA Ops:
  2.4 2.3 %collective-permute-start.5 = (f32[2,2,16,128]{3,2,1,0:T(8,128)S(1)}, f32[2,2,16,128]{3,2,1,0:T(8,128)S(1)}, u32[]{:S(2)}, u32[]{:S(2)}) collective-permute-start(f32[2,2,16,128]{3,2,1,0:T(8,128)S(1)} %get-tuple-element.33), channel_id=1, source_target_pairs={{0,2},{2,0},{4,6},{6,4},{8,10},{10,8},{12,14},{14,12},{16,18},{18,... | collective-permute-start | bytes 98312 | tf_op jit(solution)/shard_map/ppermute | solution.py:464
  4.7 3.0 %collective-permute-start.6 = (f32[2,2,16,128]{3,2,1,0:T(8,128)S(1)}, f32[2,2,16,128]{3,2,1,0:T(8,128)S(1)}, u32[]{:S(2)}, u32[]{:S(2)}) collective-permute-start(f32[2,2,16,128]{3,2,1,0:T(8,128)S(1)} %shard_map.98), channel_id=1, source_target_pairs={{0,16},{2,18},{4,20},{6,22},{8,24},{10,26},{12,28},{14,30},{16,0},... | collective-permute-start | bytes 98312 | tf_op jit(solution)/shard_map/ppermute | solution.py:464
  8.0 3.4 %collective-permute-start.7 = (f32[2,64,128]{2,1,0:T(8,128)S(1)}, f32[2,64,128]{2,1,0:T(8,128)S(1)}, u32[]{:S(2)}, u32[]{:S(2)}) collective-permute-start(f32[2,64,128]{2,1,0:T(8,128)S(1)} %shard_map.99), channel_id=1, source_target_pairs={{0,32},{2,34},{4,36},{6,38},{8,40},{10,42},{12,44},{14,46},{16,48}... | collective-permute-start | bytes 196616 | tf_op jit(solution)/shard_map/ppermute | solution.py:464
  11.3 12.7 %collective-permute-start.8 = (f32[2,64,128]{2,1,0:T(8,128)S(1)}, f32[2,64,128]{2,1,0:T(8,128)S(1)}, u32[]{:S(2)}, u32[]{:S(2)}) collective-permute-start(f32[2,64,128]{2,1,0:T(8,128)S(1)} %add.9), channel_id=1, source_target_pairs={{0,96},{2,98},{4,100},{6,102},{8,104},{10,106},{12,108},{14,110},{... | collective-permute-start | bytes 196616 | tf_op jit(solution)/shard_map/ppermute | solution.py:464
  15.0 34.9 %collective-permute-start.4 = (f32[45,16,128]{2,1,0:T(8,128)S(1)}, f32[45,16,128]{2,1,0:T(8,128)S(1)}, u32[]{:S(2)}, u32[]{:S(2)}) collective-permute-start(f32[45,16,128]{2,1,0:T(8,128)S(1)} %get-tuple-element.28), channel_id=1, source_target_pairs={{0,1},{1,0},{2,3},{3,2},{4,5},{5,4},{6,7},{7,6},{8,9},{9,8},{10,11... | collective-permute-start | bytes 1105928 | tf_op jit(solution)/shard_map/ppermute | solution.py:526
  17.8 32.1 %collective-permute-start.1 = (f32[90,8,128]{2,1,0:T(8,128)S(1)}, f32[90,8,128]{2,1,0:T(8,128)S(1)}, u32[]{:S(2)}, u32[]{:S(2)}) collective-permute-start(f32[90,8,128]{2,1,0:T(8,128)S(1)} %get-tuple-element.26), channel_id=1, source_target_pairs={{0,0},{2,4},{4,2},{6,8},{8,6},{10,12},{12,10},{14,16},{16,14},{18,... | collective-permute-start | bytes 1105928 | tf_op jit(solution)/shard_map/ppermute | solution.py:469
  24.0 25.9 %collective-permute-start = (f32[90,8,128]{2,1,0:T(8,128)S(1)}, f32[90,8,128]{2,1,0:T(8,128)S(1)}, u32[]{:S(2)}, u32[]{:S(2)}) collective-permute-start(f32[90,8,128]{2,1,0:T(8,128)S(1)} %get-tuple-element.26), channel_id=1, source_target_pairs={{0,2},{2,0},{4,6},{6,4},{8,10},{10,8},{12,14},{14,12},{16,18},{18,... | collective-permute-start | bytes 1105928 | tf_op jit(solution)/shard_map/ppermute | solution.py:464
  24.1 7.8 %collective-permute-start.9 = (f32[2,64,128]{2,1,0:T(8,128)S(1)}, f32[2,64,128]{2,1,0:T(8,128)S(1)}, u32[]{:S(2)}, u32[]{:S(2)}) collective-permute-start(f32[2,64,128]{2,1,0:T(8,128)S(1)} %add.10), channel_id=1, source_target_pairs={{0,12},{2,14},{4,8},{6,10},{8,4},{10,6},{12,0},{14,2},{16,28},{18,... | collective-permute-start | bytes 196616 | tf_op jit(solution)/shard_map/ppermute | solution.py:464
  31.9 3.3 %collective-permute-start.10 = (f32[2,64,128]{2,1,0:T(8,128)S(1)}, f32[2,64,128]{2,1,0:T(8,128)S(1)}, u32[]{:S(2)}, u32[]{:S(2)}) collective-permute-start(f32[2,64,128]{2,1,0:T(8,128)S(1)} %add.11.m0), channel_id=1, source_target_pairs={{0,4},{2,6},{4,0},{6,2},{8,12},{10,14},{12,8},{14,10},{16,20},{18,... | collective-permute-start | bytes 196616 | tf_op jit(solution)/shard_map/ppermute | solution.py:464
  35.5 2.8 %collective-permute-start.11 = (f32[2,2,16,128]{3,2,1,0:T(8,128)S(1)}, f32[2,2,16,128]{3,2,1,0:T(8,128)S(1)}, u32[]{:S(2)}, u32[]{:S(2)}) collective-permute-start(f32[2,2,16,128]{3,2,1,0:T(8,128)S(1)} %get-tuple-element.37), channel_id=1, source_target_pairs={{0,16},{2,18},{4,20},{6,22},{8,24},{10,26},{12,28},{14,30},{16,0},... | collective-permute-start | bytes 98312 | tf_op jit(solution)/shard_map/ppermute | solution.py:464
  36.0 3.0 %collective-permute-start.3 = (f32[45,8,128]{2,1,0:T(8,128)S(1)}, f32[45,8,128]{2,1,0:T(8,128)S(1)}, u32[]{:S(2)}, u32[]{:S(2)}) collective-permute-start(f32[45,8,128]{2,1,0:T(8,128)S(1)} %get-tuple-element.27), channel_id=1, source_target_pairs={{0,56},{2,2},{4,60},{6,6},{8,8},{10,10},{12,12},{14,14},{16,16},{1... | collective-permute-start | bytes 552968 | tf_op jit(solution)/shard_map/ppermute | solution.py:469
  38.3 11.5 %collective-permute-start.2 = (f32[45,8,128]{2,1,0:T(8,128)S(1)}, f32[45,8,128]{2,1,0:T(8,128)S(1)}, u32[]{:S(2)}, u32[]{:S(2)}) collective-permute-start(f32[45,8,128]{2,1,0:T(8,128)S(1)} %get-tuple-element.27), channel_id=1, source_target_pairs={{0,64},{2,2},{4,68},{6,6},{8,8},{10,10},{12,12},{14,14},{16,16},{1... | collective-permute-start | bytes 552968 | tf_op jit(solution)/shard_map/ppermute | solution.py:469
  39.0 16.1 %collective-permute-start.12 = (f32[2,2,16,128]{3,2,1,0:T(8,128)S(1)}, f32[2,2,16,128]{3,2,1,0:T(8,128)S(1)}, u32[]{:S(2)}, u32[]{:S(2)}) collective-permute-start(f32[2,2,16,128]{3,2,1,0:T(8,128)S(1)} %shard_map.102), channel_id=1, source_target_pairs={{0,2},{2,0},{4,6},{6,4},{8,10},{10,8},{12,14},{14,12},{16,18},{18,... | collective-permute-start | bytes 98312 | tf_op jit(solution)/shard_map/ppermute | solution.py:464
